TPU v7x, 128 devices: a whole 4x4x4 slice. The times are simulated.
128 devices in a mesh: ctx: 32 (over x, y, z_hi), head: 4 (over z_lo, core).
Axes of the slice: x: 4, y: 4, z: 4 (z_hi: 2, z_lo: 2; z = z_hi * 2 + z_lo), core: 2. Of those that a mesh axis runs over, the one named last changes fastest.
Arguments:
- hidden: bfloat16 [16384, 5376], P('ctx'), may hold values from -18 to 18
- w_query: bfloat16 [5376, 2048], P(None, 'head'), may hold values from -0.078125 to 0.078125
- key_weight_matrix: bfloat16 [5376, 1024], P(None, 'head'), may hold values from -0.078125 to 0.078125
- value_weight_matrix: bfloat16 [5376, 1024], P(None, 'head'), may hold values from -0.078125 to 0.078125
- attention_output_gradient: bfloat16 [16384, 2048], P('ctx', 'head'), may hold values from -6 to 6
- doc_start: int32 [16384], P('ctx'), may hold values from 0 to 16383, as said below
Outputs:
- d_hidden: float32 [16384, 5376], P(('ctx', 'head'))
Inputs may be any that keep to these rules, and one draw needn't show every extreme that they name: doc_start is non-decreasing, doc_start[i] <= i, constant within a document and equal to i at a document's first token; doc_start[0] = 0, and the last token begins a document of its own.
All inputs are finite; a program needn't handle non-finite values.
Results may differ from a plain program's by a relative error of at most 0.014.
The roundings to bfloat16 on the way count: a program that leaves them out, or rounds other values in their place, can miss the bound.
Values may be sent and summed in bfloat16 or wider, within the bound.
A program may use at most 128 MiB of HBM per device.

v0:
```python
import jax
import jax.numpy as jnp
from jax import lax
from jax.sharding import PartitionSpec as P

HEAD_SIZE = 128
W = 1024
HALO = 2


SCALE = 168.0 ** (-0.5)


def from_behind(array, axis, by):
    devices = lax.axis_size(axis)
    pairs = [(i, i + by) for i in range(devices) if 0 <= i + by < devices]
    return lax.ppermute(array, axis, pairs)


def back_project(grad, weight):
    return lax.dot_general(
        grad, weight, (((1,), (1,)), ((), ())), preferred_element_type=jnp.float32
    )


def segment_scores(query_four, key_tile_block, query_position, lower_bound, key_position):
    scores = (
        jnp.einsum("ikgd,jkd->kgij", query_four, key_tile_block, preferred_element_type=jnp.float32)
        * SCALE
    )
    allowed = (key_position[None, :] >= lower_bound[:, None]) & (
        key_position[None, :] <= query_position[:, None]
    )
    return jnp.where(allowed[None, None], scores, -jnp.inf)


def shards(
    hidden, w_query, key_weight_matrix, value_weight_matrix, attention_output_gradient, doc_start
):
    row_count = hidden.shape[0]
    kv_local = key_weight_matrix.shape[1] // HEAD_SIZE
    query_group_count = w_query.shape[1] // key_weight_matrix.shape[1]
    kv_width = kv_local * HEAD_SIZE
    leading_row = lax.axis_index("ctx") * row_count
    query_rows = jnp.dot(hidden, w_query, preferred_element_type=jnp.float32).astype(jnp.bfloat16)
    projected_keys = jnp.dot(hidden, key_weight_matrix, preferred_element_type=jnp.float32).astype(
        jnp.bfloat16
    )
    projected_values = jnp.dot(
        hidden, value_weight_matrix, preferred_element_type=jnp.float32
    ).astype(jnp.bfloat16)
    packed = jnp.concatenate([projected_keys, projected_values], axis=1)
    earlier = []
    moving = packed
    for distance in range(HALO):
        moving = from_behind(moving, "ctx", 1)
        earlier.append(moving)
    query_position = leading_row + jnp.arange(row_count, dtype=jnp.int32)
    lower_bound = jnp.maximum(doc_start, query_position - W + 1)
    query_four = query_rows.reshape(row_count, kv_local, query_group_count, HEAD_SIZE)
    output_gradient = attention_output_gradient.reshape(
        row_count, kv_local, query_group_count, HEAD_SIZE
    )
    ordered = earlier[::-1] + [packed]
    halo_first = leading_row - HALO * row_count
    segments = [jnp.concatenate(ordered, axis=0)]
    seg_firsts = [halo_first]
    key_blocks = []
    value_blocks = []
    score_list = []
    for segment, seg_first in zip(segments, seg_firsts):
        seg_rows = segment.shape[0]
        key_tile_block = segment[:, :kv_width].reshape(seg_rows, kv_local, HEAD_SIZE)
        value_tile_block = segment[:, kv_width:].reshape(seg_rows, kv_local, HEAD_SIZE)
        key_position = seg_first + jnp.arange(seg_rows, dtype=jnp.int32)
        key_blocks.append(key_tile_block)
        value_blocks.append(value_tile_block)
        score_list.append(
            segment_scores(query_four, key_tile_block, query_position, lower_bound, key_position)
        )
    row_max = score_list[0].max(axis=-1)
    scores = score_list[0]
    denominator = jnp.sum(jnp.exp(scores - row_max[..., None]), axis=-1)
    log_total = row_max + jnp.log(denominator)
    prob_list = []
    output = jnp.zeros((row_count, kv_local, query_group_count, HEAD_SIZE), jnp.float32)
    for scores, value_tile_block in zip(score_list, value_blocks):
        probability = jnp.exp(scores - log_total[..., None])
        probability_low = probability.astype(jnp.bfloat16)
        prob_list.append((probability, probability_low))
        output = jnp.einsum(
            "kgij,jkd->ikgd", probability_low, value_tile_block, preferred_element_type=jnp.float32
        )
    row_dot = jnp.einsum("ikgd,ikgd->kgi", output_gradient.astype(jnp.float32), output)
    d_query = jnp.zeros((row_count, kv_local, query_group_count, HEAD_SIZE), jnp.float32)
    grad_list = []
    for (probability, probability_low), key_tile_block, value_tile_block in zip(
        prob_list, key_blocks, value_blocks
    ):
        d_probs = jnp.einsum(
            "ikgd,jkd->kgij", output_gradient, value_tile_block, preferred_element_type=jnp.float32
        )
        d_scores = (probability * (d_probs - row_dot[..., None]) * SCALE).astype(jnp.bfloat16)
        d_query = jnp.einsum(
            "kgij,jkd->ikgd", d_scores, key_tile_block, preferred_element_type=jnp.float32
        )
        d_key = jnp.einsum(
            "kgij,ikgd->jkd", d_scores, query_four, preferred_element_type=jnp.float32
        )
        d_value = jnp.einsum(
            "kgij,ikgd->jkd", probability_low, output_gradient, preferred_element_type=jnp.float32
        )
        seg_rows = key_tile_block.shape[0]
        grad_list.append(
            jnp.concatenate(
                [d_key.reshape(seg_rows, kv_width), d_value.reshape(seg_rows, kv_width)], axis=1
            )
        )
    full_grad = grad_list[0]
    own_grad = full_grad[HALO * row_count :]
    passing = jnp.zeros_like(own_grad)
    for distance in range(HALO, 0, -1):
        passing = from_behind(
            passing + full_grad[(HALO - distance) * row_count : (HALO - distance + 1) * row_count],
            "ctx",
            -1,
        )
    combined = own_grad + passing
    d_query_low = d_query.reshape(row_count, kv_local * query_group_count * HEAD_SIZE).astype(
        jnp.bfloat16
    )
    key_gradient_rows = combined[:, :kv_width].astype(jnp.bfloat16)
    value_gradient_rows = combined[:, kv_width:].astype(jnp.bfloat16)
    contribution = back_project(d_query_low, w_query)
    contribution = contribution + back_project(key_gradient_rows, key_weight_matrix)
    return lax.psum_scatter(
        contribution + back_project(value_gradient_rows, value_weight_matrix),
        "head",
        scatter_dimension=0,
        tiled=True,
    )


def solution(mesh):
    in_specs = (
        P("ctx", None),
        P(None, "head"),
        P(None, "head"),
        P(None, "head"),
        P("ctx", "head"),
        P("ctx"),
    )
    out_specs = P(("ctx", "head"), None)
    return jax.shard_map(shards, mesh=mesh, in_specs=in_specs, out_specs=out_specs, check_vma=False)
```

profile of v0, /device:TPU:95, one launch (start us, length us, event | category | flops | bytes accessed | tf_op | source)
XLA Modules:
  0.0 278.3 jit_solution(2153470300938520847)
XLA Ops:
  6.5 1.8 copy-done
  8.3 4.3 %convolution_convert_fusion.3 = bf16[512,256]{0,1:T(8,128)(2,1)S(1)} fusion(bf16[512,5376]{1,0:T(8,128)(2,1)} %param.6, bf16[5376,256]{1,0:T(8,128)(2,1)S(1)} %copy-done), kind=kOutput, calls=%fused_computation.19 | convolution fusion | flops 1409417216 | bytes 8519680 | tf_op jit(solution)/shard_map/dot_general | solution.py:46
  12.7 4.7 %convolution_convert_fusion.2 = bf16[512,256]{0,1:T(8,128)(2,1)S(1)} fusion(bf16[512,5376]{1,0:T(8,128)(2,1)} %param.6, bf16[5376,256]{1,0:T(8,128)(2,1)S(1)} %copy-done.8), kind=kOutput, calls=%fused_computation.18 | convolution fusion | flops 1409417216 | bytes 8519680 | tf_op jit(solution)/shard_map/dot_general | solution.py:49
  18.1 1.3 collective-permute-start
  19.5 3.9 %convolution_convert_fusion.1 = bf16[512,512]{0,1:T(8,128)(2,1)} fusion(bf16[512,5376]{1,0:T(8,128)(2,1)S(1)} %bitcast.100, bf16[5376,512]{1,0:T(8,128)(2,1)S(1)} %bitcast.89), kind=kOutput, calls=%fused_computation.17 | convolution fusion | flops 2818834432 | bytes 11534336 | tf_op jit(solution)/shard_map/dot_general | solution.py:45
  23.4 11.1 %collective-permute-done = bf16[512,512]{0,1:T(8,128)(2,1)} collective-permute-done((bf16[512,512]{0,1:T(8,128)(2,1)S(1)}, bf16[512,512]{0,1:T(8,128)(2,1)}, u32[]{:S(2)}, u32[]{:S(2)}) %collective-permute-start) | collective-permute-done | bytes 524320 | tf_op jit(solution)/shard_map/ppermute | solution.py:17
  34.5 1.5 collective-permute-start.1
  35.9 1.2 reshape.93
  37.1 1.4 copy.14
  39.2 10.9 %collective-permute-done.1 = bf16[512,512]{0,1:T(8,128)(2,1)} collective-permute-done((bf16[512,512]{0,1:T(8,128)(2,1)}, bf16[512,512]{0,1:T(8,128)(2,1)}, u32[]{:S(2)}, u32[]{:S(2)}) %collective-permute-start.1) | collective-permute-done | bytes 524320 | tf_op jit(solution)/shard_map/ppermute | solution.py:17
  50.1 1.4 maximum_maximum_fusion
  51.6 2.4 fusion.4
  54.0 2.7 exponential_reduce_fusion
  56.8 1.7 copy-done.3
  58.5 4.3 %fusion.16 = f32[2,128,2,512]{3,1,2,0:T(8,128)} fusion(bf16[1536,2,128,1]{0,2,3,1:T(8,128)(2,1)S(1)} %bitcast.95, f32[2,1536,512,2]{2,1,3,0:T(8,128)S(1)} %get-tuple-element.8, f32[2,2,512]{2,1,0:T(2,128)S(1)} %log_add_fusion, pred[512,1536]{0,1:T(8,128)(4,1)S(1)} %compare_and_fusion), kind=kOutput, calls=%fused_computation.37 | convolution fusion | flops 817889280 | bytes 15212544 | tf_op jit(solution)/shard_map/kgij,jkd->ikgd/dot_general | solution.py:91
  62.9 2.3 copy.38
  65.1 3.5 %fusion.10 = f32[2,2,512]{1,0,2:T(2,128)} fusion(f32[2,128,2,512]{1,2,0,3:T(2,128)} %copy.38, bf16[512,2,2,128]{3,2,1,0:T(2,128)(2,1)S(1)} %reshape.93), kind=kLoop, calls=%fused_computation.27 | loop fusion | flops 784384 | bytes 1581056
  68.6 1.2 copy.26
  69.9 8.3 %fusion.14 = f32[2,1536,128,1]{1,2,3,0:T(8,128)S(1)} fusion(bf16[512,2,2,128]{0,3,2,1:T(8,128)(2,1)} %copy.14, f32[2,1536,512,2]{2,1,3,0:T(8,128)} %copy-done.3, f32[2,2,512]{2,1,0:T(2,128)S(1)} %log_add_fusion, pred[512,1536]{0,1:T(8,128)(4,1)} %copy-done.4), kind=kOutput, calls=%fused_computation.36 | convolution fusion | flops 817889280 | bytes 15474688 | tf_op jit(solution)/shard_map/kgij,ikgd->jkd/dot_general | solution.py:110
  78.3 8.3 %fusion.2 = bf16[2,2,512,1536]{2,3,1,0:T(8,128)(2,1)S(1)} fusion(f32[2,1536,512,2]{2,1,3,0:T(8,128)} %copy-done.3, bf16[1536,2,128,1]{0,2,3,1:T(8,128)(2,1)S(1)} %bitcast.96, bf16[512,2,2,128]{0,3,2,1:T(8,128)(2,1)S(1)} %copy-done.14, f32[2,2,512]{2,1,0:T(2,128)S(1)} %copy.26, f32[2,2,512]{2,1,0:T(2,128)S(1)} %log_add_fusion, pred[512,1536]{0,1:T(8,128)(4,1)S(1)} %copy-done.5), kind=kOutput, calls=%fused_computation.3 | convolution fusion | flops 827326464 | bytes 20987904 | tf_op jit(solution)/shard_map/ikgd,jkd->kgij/dot_general | solution.py:100
  86.6 2.1 fusion.20
  88.8 3.4 %collective-permute-start.2 = (f32[512,512]{0,1:T(8,128)S(1)}, f32[512,512]{0,1:T(8,128)S(1)}, u32[]{:S(2)}, u32[]{:S(2)}) collective-permute-start(f32[512,512]{0,1:T(8,128)S(1)} %fusion.5), channel_id=1, source_target_pairs={{4,0},{8,4},{12,8},{16,12},{20,16},{24,20},{28,24},{32,28},{36,32}... | collective-permute-start | bytes 3145736 | tf_op jit(solution)/shard_map/ppermute | solution.py:17
  92.2 20.0 %collective-permute-done.2 = f32[512,512]{0,1:T(8,128)S(1)} collective-permute-done((f32[512,512]{0,1:T(8,128)S(1)}, f32[512,512]{0,1:T(8,128)S(1)}, u32[]{:S(2)}, u32[]{:S(2)}) %collective-permute-start.2) | collective-permute-done | bytes 1048608 | tf_op jit(solution)/shard_map/ppermute | solution.py:17
  112.3 1.2 fusion.9
  113.5 6.7 %collective-permute-start.3 = (f32[512,512]{0,1:T(8,128)}, f32[512,512]{0,1:T(8,128)}, u32[]{:S(2)}, u32[]{:S(2)}) collective-permute-start(f32[512,512]{0,1:T(8,128)} %fusion.9), channel_id=1, source_target_pairs={{4,0},{8,4},{12,8},{16,12},{20,16},{24,20},{28,24},{32,28},{36,32}... | collective-permute-start | bytes 3145736 | tf_op jit(solution)/shard_map/ppermute | solution.py:17
  120.2 1.0 convolution_convert_fusion
  121.3 3.1 %fusion.19 = f32[512,5376]{1,0:T(8,128)S(1)} fusion(bf16[512,512]{0,1:T(8,128)(2,1)S(1)} %bitcast.94, bf16[5376,512]{1,0:T(8,128)(2,1)S(1)} %bitcast.91), kind=kOutput, calls=%fused_computation.39 | convolution fusion | flops 2818572288 | bytes 17039360 | tf_op jit(solution)/shard_map/dot_general | solution.py:21
  124.3 14.5 %collective-permute-done.3 = f32[512,512]{0,1:T(8,128)} collective-permute-done((f32[512,512]{0,1:T(8,128)}, f32[512,512]{0,1:T(8,128)}, u32[]{:S(2)}, u32[]{:S(2)}) %collective-permute-start.3) | collective-permute-done | bytes 1048608 | tf_op jit(solution)/shard_map/ppermute | solution.py:17
  138.8 1.4 fusion.8
  140.2 5.9 %fusion.12 = f32[512,5376]{1,0:T(8,128)} fusion(bf16[5376,256]{1,0:T(8,128)(2,1)S(1)} %copy-done, bf16[512,512]{0,1:T(8,128)(2,1)S(1)} %fusion.8), kind=kOutput, calls=%fused_computation.30 | convolution fusion | flops 1409286144 | bytes 14024704 | tf_op jit(solution)/shard_map/dot_general | solution.py:21
  146.1 10.8 %add_add_fusion = f32[512,5376]{1,0:T(8,128)} fusion(f32[512,5376]{1,0:T(8,128)S(1)} %fusion.19, f32[512,5376]{1,0:T(8,128)} %fusion.12, bf16[5376,256]{1,0:T(8,128)(2,1)} %param.9, bf16[512,512]{0,1:T(8,128)(2,1)S(1)} %fusion.8), kind=kOutput, calls=%fused_computation.8 | convolution fusion | flops 1414791168 | bytes 36044800 | tf_op jit(solution)/shard_map/dot_general | solution.py:21
  156.9 114.6 %reduce-scatter.2.cloned.1.call-done = f32[128,5376]{1,0:T(8,128)} async-done(((f32[512,5376]{1,0:T(8,128)}), f32[128,5376]{1,0:T(8,128)}) %reduce-scatter.2.cloned.1.call-update) | async-done | bytes 2752528 | tf_op jit(solution)/shard_map/reduce_scatter | solution.py:136
  (54 shorter events, 1.7 us)
Async XLA Ops:
  6.5 1.8 copy-start
  6.5 265.0 %reduce-scatter.2.cloned.1.call-start = ((), (), s32[]{:S(2)}) async-start(), calls=%async_computation.1 | async-start | bytes 13762560 | tf_op jit(solution)/shard_map/reduce_scatter | solution.py:136
  8.3 4.4 %copy-start.8 = (bf16[5376,256]{1,0:T(8,128)(2,1)S(1)}, bf16[5376,256]{1,0:T(8,128)(2,1)}, u32[]{:S(2)}) copy-start(bf16[5376,256]{1,0:T(8,128)(2,1)} %param.9) | copy-start | bytes 8257540
  8.3 11.1 %slice-start = ((s8[5505024]{0:T(1024)(128)(4,1)}), s8[4194304]{0:T(1024)(128)(4,1)S(1)}, s32[]{:S(2)}) async-start(s8[5505024]{0:T(1024)(128)(4,1)} %bitcast.88), calls=%async_computation.2 | async-start | bytes 8388608
  8.3 11.1 %slice-start.4 = ((s8[5505024]{0:T(1024)(128)(4,1)}), s8[4194304]{0:T(1024)(128)(4,1)S(1)}, s32[]{:S(2)}) async-start(s8[5505024]{0:T(1024)(128)(4,1)} %bitcast.99), calls=%async_computation.6 | async-start | bytes 8388608
  12.7 6.8 %slice-start.1 = ((s8[5505024]{0:T(1024)(128)(4,1)}), s8[1310720]{0:T(1024)(128)(4,1)S(1)}, s32[]{:S(2)}) async-start(s8[5505024]{0:T(1024)(128)(4,1)} %bitcast.88), calls=%async_computation.3 | async-start | bytes 2621440
  12.7 6.8 %slice-start.5 = ((s8[5505024]{0:T(1024)(128)(4,1)}), s8[1310720]{0:T(1024)(128)(4,1)S(1)}, s32[]{:S(2)}) async-start(s8[5505024]{0:T(1024)(128)(4,1)} %bitcast.99), calls=%async_computation.7 | async-start | bytes 2621440
  17.4 0.7 copy-start.9
  18.1 5.2 %copy-start.15 = (s32[512]{0:T(512)S(1)}, s32[512]{0:T(512)}, u32[]{:S(2)}) copy-start(s32[512]{0:T(512)} %param.11) | copy-start | bytes 6148
  18.1 16.3 %collective-permute-start = (bf16[512,512]{0,1:T(8,128)(2,1)S(1)}, bf16[512,512]{0,1:T(8,128)(2,1)}, u32[]{:S(2)}, u32[]{:S(2)}) collective-permute-start(bf16[512,512]{0,1:T(8,128)(2,1)S(1)} %pad_maximum_fusion.1), channel_id=1, source_target_pairs={{0,4},{4,8},{8,12},{12,16},{16,20},{20,24},{24,28},{28,32},{32,36}... | collective-permute-start | bytes 1572872 | tf_op jit(solution)/shard_map/ppermute | solution.py:17
  34.5 15.7 %collective-permute-start.1 = (bf16[512,512]{0,1:T(8,128)(2,1)}, bf16[512,512]{0,1:T(8,128)(2,1)}, u32[]{:S(2)}, u32[]{:S(2)}) collective-permute-start(bf16[512,512]{0,1:T(8,128)(2,1)} %collective-permute-done), channel_id=1, source_target_pairs={{0,4},{4,8},{8,12},{12,16},{16,20},{20,24},{24,28},{28,32},{32,36}... | collective-permute-start | bytes 1572872 | tf_op jit(solution)/shard_map/ppermute | solution.py:17
  38.5 13.1 %copy-start.12 = (bf16[512,512]{0,1:T(8,128)(2,1)S(1)}, bf16[512,512]{0,1:T(8,128)(2,1)}, u32[]{:S(2)}) copy-start(bf16[512,512]{0,1:T(8,128)(2,1)} %convolution_convert_fusion.1) | copy-start | bytes 1572868
  39.2 17.6 %copy-start.4 = (pred[512,1536]{0,1:T(8,128)(4,1)}, pred[512,1536]{0,1:T(8,128)(4,1)S(1)}, u32[]{:S(2)}) copy-start(pred[512,1536]{0,1:T(8,128)(4,1)S(1)} %compare_and_fusion) | copy-start | bytes 2359300
  51.6 2.4 copy-start.6
  51.6 5.2 %copy-start.10 = (bf16[1536,256]{0,1:T(8,128)(2,1)}, bf16[1536,256]{0,1:T(8,128)(2,1)S(1)}, u32[]{:S(2)}) copy-start(bf16[1536,256]{0,1:T(8,128)(2,1)S(1)} %get-tuple-element.5) | copy-start | bytes 2359300
  54.0 4.5 %copy-start.3 = (f32[2,1536,512,2]{2,1,3,0:T(8,128)}, f32[2,1536,512,2]{2,1,3,0:T(8,128)S(1)}, u32[]{:S(2)}) copy-start(f32[2,1536,512,2]{2,1,3,0:T(8,128)S(1)} %get-tuple-element.8) | copy-start | bytes 37748740
  69.8 8.4 %copy-start.5 = (pred[512,1536]{0,1:T(8,128)(4,1)S(1)}, pred[512,1536]{0,1:T(8,128)(4,1)}, u32[]{:S(2)}) copy-start(pred[512,1536]{0,1:T(8,128)(4,1)} %copy-done.4) | copy-start | bytes 2359300
  69.9 8.4 %copy-start.11 = (bf16[1536,256]{0,1:T(8,128)(2,1)S(1)}, bf16[1536,256]{0,1:T(8,128)(2,1)}, u32[]{:S(2)}) copy-start(bf16[1536,256]{0,1:T(8,128)(2,1)} %copy-done.10) | copy-start | bytes 2359300
  69.9 8.4 %copy-start.14 = (bf16[512,2,2,128]{0,3,2,1:T(8,128)(2,1)S(1)}, bf16[512,2,2,128]{0,3,2,1:T(8,128)(2,1)}, u32[]{:S(2)}) copy-start(bf16[512,2,2,128]{0,3,2,1:T(8,128)(2,1)} %copy.14) | copy-start | bytes 1572868
  78.2 34.0 %copy-start.1 = (f32[2,1536,128,1]{1,2,3,0:T(8,128)}, f32[2,1536,128,1]{1,2,3,0:T(8,128)S(1)}, u32[]{:S(2)}) copy-start(f32[2,1536,128,1]{1,2,3,0:T(8,128)S(1)} %fusion.14) | copy-start | bytes 4718596
  78.3 8.3 %copy-start.13 = (bf16[512,512]{0,1:T(8,128)(2,1)S(1)}, bf16[512,512]{0,1:T(8,128)(2,1)}, u32[]{:S(2)}) copy-start(bf16[512,512]{0,1:T(8,128)(2,1)} %convolution_convert_fusion.1) | copy-start | bytes 1572868
  88.7 31.5 %copy-start.7 = (bf16[1536,256]{0,1:T(8,128)(2,1)S(1)}, bf16[1536,256]{0,1:T(8,128)(2,1)}, u32[]{:S(2)}) copy-start(bf16[1536,256]{0,1:T(8,128)(2,1)} %copy-done.6) | copy-start | bytes 2359300
  88.8 32.4 %slice-start.2 = ((s8[5505024]{0:T(1024)(128)(4,1)}), s8[4194304]{0:T(1024)(128)(4,1)S(1)}, s32[]{:S(2)}) async-start(s8[5505024]{0:T(1024)(128)(4,1)} %bitcast.90), calls=%async_computation.4 | async-start | bytes 8388608
  88.8 23.4 %collective-permute-start.2 = (f32[512,512]{0,1:T(8,128)S(1)}, f32[512,512]{0,1:T(8,128)S(1)}, u32[]{:S(2)}, u32[]{:S(2)}) collective-permute-start(f32[512,512]{0,1:T(8,128)S(1)} %fusion.5), channel_id=1, source_target_pairs={{4,0},{8,4},{12,8},{16,12},{20,16},{24,20},{28,24},{32,28},{36,32}... | collective-permute-start | bytes 3145736 | tf_op jit(solution)/shard_map/ppermute | solution.py:17
  113.5 7.7 %slice-start.3 = ((s8[5505024]{0:T(1024)(128)(4,1)}), s8[1310720]{0:T(1024)(128)(4,1)S(1)}, s32[]{:S(2)}) async-start(s8[5505024]{0:T(1024)(128)(4,1)} %bitcast.90), calls=%async_computation.5 | async-start | bytes 2621440
  113.5 25.3 %collective-permute-start.3 = (f32[512,512]{0,1:T(8,128)}, f32[512,512]{0,1:T(8,128)}, u32[]{:S(2)}, u32[]{:S(2)}) collective-permute-start(f32[512,512]{0,1:T(8,128)} %fusion.9), channel_id=1, source_target_pairs={{4,0},{8,4},{12,8},{16,12},{20,16},{24,20},{28,24},{32,28},{36,32}... | collective-permute-start | bytes 3145736 | tf_op jit(solution)/shard_map/ppermute | solution.py:17
  121.2 17.6 %copy-start.2 = (f32[2,1536,128,1]{1,2,3,0:T(8,128)S(1)}, f32[2,1536,128,1]{1,2,3,0:T(8,128)}, u32[]{:S(2)}) copy-start(f32[2,1536,128,1]{1,2,3,0:T(8,128)} %copy-done.1) | copy-start | bytes 4718596
Sparse Core Ops, SparseCore 0:
  157.1 114.3 reduce-scatter.1
where the time goes:
time: 281 us; the launch traced here: 278 us
  waiting for transfers between devices  171 us (61%)
  matrix products  59.1 us (21%)
  between operations  13.8 us (5%)
  starting transfers between devices  12.9 us (5%)
  other arithmetic  11 us (4%)
  local copies, waits for them, and re-layouts  10.5 us (4%)
    reduce_scatter x1, waiting for transfers between devices, shards(): lax.psum_scatter(contribution + back_project(value_gradient_rows, value_w...  115 us
    ppermute x4, waiting for transfers between devices, from_behind(): return lax.ppermute(array, axis, pairs)  56.5 us
    dot_general x3, matrix products, back_project(): lax.dot_general(grad, weight, (((1,), (1,)), ((), ())), preferred_element...  19.8 us
    ppermute x4, starting transfers between devices, from_behind(): return lax.ppermute(array, axis, pairs)  12.9 us
    dot_general x1, matrix products, shards(): jnp.einsum('kgij,ikgd->jkd', probability_low, output_gradient, preferred_...  8.34 us
    dot_general x1, matrix products, shards(): jnp.einsum('ikgd,jkd->kgij', output_gradient, value_tile_block, preferred...  8.32 us
    unnamed x45, local copies, waits for them, and re-layouts  6.56 us
  transfers between devices with their start and end apart: 5, of which 5 were waited for; matrix products, arithmetic and copies ran while one was open for 4% of the time, Pallas kernels for 0%

commit v1 on v0

v1 whole, which is shorter than its diff:
```python
import functools
import math

import jax
import jax.numpy as jnp
from jax import lax
from jax.experimental import pallas as pl
from jax.experimental.pallas import tpu as pltpu
from jax.sharding import PartitionSpec as P

HEAD = 128
WINDOW = 1024
SCALE = 168.0 ** (-0.5)
LOG2E = math.log2(math.e)
MESH = pl.DeviceIdType.MESH
F32 = jnp.float32
BF16 = jnp.bfloat16

TOK = 512
QT = 256
KEYS = 1280
STRIP = 32
NT = (((1,), (1,)), ((), ()))
TN = (((0,), (0,)), ((), ()))


def kernel(
    n_ctx, kcn, kc, ncn, nc,
    hid, wq, wk, wv, dog, doc, out,
    h, wall, acc, kv, q, do, lo, s, dp, pw, ds, dkv, dkv_out, dkv_in, grad,
    rs1_out, rs1_in, rs2_out, rs2_in, other, keep,
    sem_h, sem_k, sem_v, sem_q, sem_do, sem_o,
    kv_ss, kv_rs, dkv_ss, dkv_rs, r1_ss, r1_rs, r2_ss, r2_rs,
):
    ctx = lax.axis_index("ctx")
    head = lax.axis_index("head")
    zpos, core = head // 2, lax.rem(head, 2)

    def at_ctx(by):
        return (lax.rem(ctx + by + n_ctx, n_ctx), head)

    next1, next2, prev1, prev2 = at_ctx(1), at_ctx(2), at_ctx(-1), at_ctx(-2)
    mate = (ctx, head + 1 - 2 * core)
    across = (ctx, lax.rem(head + 2, 4))

    barrier = pltpu.get_barrier_semaphore()
    for peer in (next1, next2, prev1, prev2, mate, across):
        pl.semaphore_signal(barrier, inc=1, device_id=peer, device_id_type=MESH)

    def cols(k):
        return pl.ds(pl.multiple_of(k * kc, 128), kc)

    def in_h(k):
        return pltpu.make_async_copy(hid.at[:, cols(k)], h.at[k], sem_h.at[k])

    def in_k(k):
        return pltpu.make_async_copy(wk.at[cols(k), :], wall.at[cols(k), pl.ds(512, 256)], sem_k.at[k])

    def in_v(k):
        return pltpu.make_async_copy(wv.at[cols(k), :], wall.at[cols(k), pl.ds(768, 256)], sem_v.at[k])

    def in_q(k):
        return pltpu.make_async_copy(wq.at[cols(k), :], wall.at[cols(k), pl.ds(0, 512)], sem_q.at[k])

    for k in range(kcn):
        in_h(k).start()
        in_k(k).start()
        in_v(k).start()
    for k in range(kcn):
        in_q(k).start()
    do_copies = []
    for g in range(2):
        for t in range(2):
            for m in range(2):
                do_copies.append(
                    pltpu.make_async_copy(
                        dog.at[pl.ds(t * QT, QT), pl.ds((2 * g + m) * HEAD, HEAD)],
                        do.at[g, t, pl.ds(m * QT, QT), :],
                        sem_do.at[4 * g + 2 * t + m],
                    )
                )
    for copy in do_copies:
        copy.start()

    first = ctx * TOK
    lane = lax.broadcasted_iota(jnp.int32, (1, TOK), 1)
    low = jnp.maximum(doc[...].reshape(1, TOK) - first + WINDOW, lane + 1)
    for t in range(2):
        part = low[:, t * QT : (t + 1) * QT] - t * QT
        lo[t] = jnp.concatenate([part, part], axis=1)

    acc[...] = jnp.zeros_like(acc)

    @pl.loop(0, kcn)
    def _(k):
        in_h(k).wait()
        in_k(k).wait()
        in_v(k).wait()
        acc[...] += jnp.dot(h[k], wall[cols(k), pl.ds(512, 512)], preferred_element_type=F32)

    for g in range(2):
        for j in range(2):
            kv[g, j, pl.ds(2 * TOK, TOK), :] = acc[:, pl.ds(j * 256 + g * HEAD, HEAD)].astype(BF16)

    pl.semaphore_wait(barrier, 6)

    def send_kv(g, far):
        return pltpu.make_async_remote_copy(
            src_ref=kv.at[g, :, pl.ds(2 * TOK, TOK), :],
            dst_ref=kv.at[g, :, pl.ds((1 - far) * TOK, TOK), :],
            send_sem=kv_ss.at[g, far],
            recv_sem=kv_rs.at[g, far],
            device_id=next2 if far else next1,
            device_id_type=MESH,
        )

    for g in range(2):
        for far in range(2):
            send_kv(g, far).start()

    acc[...] = jnp.zeros_like(acc)

    @pl.loop(0, kcn)
    def _(k):
        in_q(k).wait()
        acc[...] += jnp.dot(h[k], wall[cols(k), pl.ds(0, 512)], preferred_element_type=F32)

    for g in range(2):
        for t in range(2):
            for m in range(2):
                q[g, t, pl.ds(m * QT, QT), :] = acc[
                    pl.ds(t * QT, QT), pl.ds((2 * g + m) * HEAD, HEAD)
                ].astype(BF16)
    for copy in do_copies:
        copy.wait()
    dkv[...] = jnp.zeros_like(dkv)

    def same(a, b):
        return 1 - (a + b - 2 * a * b)

    def place(b):
        return pl.multiple_of(128 * (2 * same(lax.rem(b, 2), core) + same(b // 2, zpos)), 128)

    def send_dkv(g, far):
        return pltpu.make_async_remote_copy(
            src_ref=dkv_out.at[g, :, pl.ds((1 - far) * TOK, TOK), :],
            dst_ref=dkv_in.at[far, g],
            send_sem=dkv_ss.at[g, far],
            recv_sem=dkv_rs.at[g, far],
            device_id=prev2 if far else prev1,
            device_id_type=MESH,
        )

    for g in range(2):
        for far in range(2):
            send_kv(g, far).wait_recv()

        @pl.loop(0, 2)
        def _(t):
            rows = pl.ds(pl.multiple_of(t * QT, QT), KEYS)
            s[...] = lax.dot_general(kv[g, 0, rows, :], q[g, t], NT, preferred_element_type=F32)
            dp[...] = lax.dot_general(kv[g, 1, rows, :], do[g, t], NT, preferred_element_type=F32)
            lowest = lo[t]
            local = lax.broadcasted_iota(jnp.int32, (STRIP, 2 * QT), 0)
            lane2 = lax.broadcasted_iota(jnp.int32, (1, QT), 1)
            highest = WINDOW + jnp.concatenate([lane2, lane2], axis=1)

            def strip(i):
                return pl.ds(pl.multiple_of(i * STRIP, STRIP), STRIP)

            def mask_inner(i, top):
                kept = jnp.where(local + i * STRIP >= lowest, s[strip(i), :], -jnp.inf)
                s[strip(i), :] = kept
                return jnp.maximum(top, kept)

            def mask_edge(i, top):
                key = local + i * STRIP
                kept = jnp.where((key >= lowest) & (key <= highest), s[strip(i), :], -jnp.inf)
                s[strip(i), :] = kept
                return jnp.maximum(top, kept)

            top = jnp.full((STRIP, 2 * QT), -jnp.inf, F32)
            top = lax.fori_loop(0, WINDOW // STRIP, mask_inner, top)
            top = lax.fori_loop(WINDOW // STRIP, KEYS // STRIP, mask_edge, top)
            top = jnp.max(top, axis=0, keepdims=True)

            def weigh(i, sums):
                total, dots = sums
                weight = jnp.exp2((s[strip(i), :] - top) * (SCALE * LOG2E))
                s[strip(i), :] = weight
                return total + weight, dots + weight * dp[strip(i), :]

            zero = jnp.zeros((STRIP, 2 * QT), F32)
            total, dots = lax.fori_loop(0, KEYS // STRIP, weigh, (zero, zero))
            inverse = 1.0 / jnp.sum(total, axis=0, keepdims=True)
            row_dot = jnp.sum(dots, axis=0, keepdims=True) * inverse

            @pl.loop(0, KEYS // STRIP)
            def _(i):
                prob = s[strip(i), :] * inverse
                pw[strip(i), :] = prob.astype(BF16)
                ds[strip(i), :] = (prob * (dp[strip(i), :] - row_dot)).astype(BF16)

            dq = lax.dot_general(kv[g, 0, rows, :], ds[...], TN, preferred_element_type=F32)
            dq = jnp.transpose(dq * SCALE).astype(BF16)
            for m in range(2):
                for j in range(2):
                    grad[pl.ds(place(2 * t + j), 128), pl.ds((2 * g + m) * HEAD, HEAD)] = dq[
                        m * QT + j * 128 : m * QT + (j + 1) * 128
                    ]
            dkv[g, 0, rows, :] += jnp.dot(ds[...], q[g, t], preferred_element_type=F32)
            dkv[g, 1, rows, :] += jnp.dot(pw[...], do[g, t], preferred_element_type=F32)

        dkv_out[g, 0] = (dkv[g, 0, pl.ds(0, 2 * TOK), :] * SCALE).astype(BF16)
        dkv_out[g, 1] = dkv[g, 1, pl.ds(0, 2 * TOK), :].astype(BF16)
        for far in range(2):
            send_dkv(g, far).start()

    for g in range(2):
        for far in range(2):
            send_dkv(g, far).wait_recv()
        for j in range(2):
            for b in range(4):
                rows = pl.ds(b * 128, 128)
                own = dkv[g, j, pl.ds(2 * TOK + b * 128, 128), :]
                if j == 0:
                    own = own * SCALE
                whole = own + (dkv_in[0, g, j, rows, :].astype(F32) + dkv_in[1, g, j, rows, :].astype(F32))
                grad[pl.ds(place(b), 128), pl.ds(512 + j * 256 + g * HEAD, HEAD)] = whole.astype(BF16)

    def send_r1(c):
        return pltpu.make_async_remote_copy(
            src_ref=rs1_out.at[c], dst_ref=rs1_in.at[c],
            send_sem=r1_ss.at[c], recv_sem=r1_rs.at[c],
            device_id=mate, device_id_type=MESH,
        )

    def send_r2(c):
        return pltpu.make_async_remote_copy(
            src_ref=rs2_out.at[c], dst_ref=rs2_in.at[c],
            send_sem=r2_ss.at[c], recv_sem=r2_rs.at[c],
            device_id=across, device_id_type=MESH,
        )

    def out_copy(c):
        return pltpu.make_async_copy(
            keep.at[c], out.at[:, pl.ds(pl.multiple_of(c * nc, nc), nc)], sem_o.at[c]
        )

    def join(c):
        send_r1(c).wait_recv()
        rs2_out[c] = (other[c] + rs1_in[c, pl.ds(0, 128), :].astype(F32)).astype(BF16)
        send_r2(c).start()
        keep[c] = keep[c] + rs1_in[c, pl.ds(128, 128), :].astype(F32)

    @pl.loop(0, ncn)
    def _(c):
        part = lax.dot_general(
            grad[...], wall[pl.ds(pl.multiple_of(c * nc, nc), nc), :], NT, preferred_element_type=F32
        )
        rs1_out[c] = part[:256].astype(BF16)
        other[c] = part[256:384]
        keep[c] = part[384:]
        send_r1(c).start()

        @pl.when(c > 0)
        def _():
            join(c - 1)

    join(ncn - 1)

    @pl.loop(0, ncn)
    def _(c):
        send_r2(c).wait_recv()
        keep[c] = keep[c] + rs2_in[c].astype(F32)
        out_copy(c).start()

    @pl.loop(0, ncn)
    def _(c):
        out_copy(c).wait()
        send_r1(c).wait_send()
        send_r2(c).wait_send()

    for g in range(2):
        for far in range(2):
            send_kv(g, far).wait_send()
            send_dkv(g, far).wait_send()


def shards(hidden, w_query, key_weight, value_weight, out_gradient, doc_start, *, n_ctx):
    width = hidden.shape[1]
    kcn = 7
    kc = width // kcn
    nc = 256
    ncn = width // nc
    dma = pltpu.SemaphoreType.DMA
    anywhere = pl.BlockSpec(memory_space=pl.ANY)
    return pl.pallas_call(
        functools.partial(kernel, n_ctx, kcn, kc, ncn, nc),
        out_shape=jax.ShapeDtypeStruct((128, width), F32),
        in_specs=[anywhere] * 5 + [pl.BlockSpec(memory_space=pltpu.VMEM)],
        out_specs=anywhere,
        scratch_shapes=[
            pltpu.VMEM((kcn, TOK, kc), BF16),
            pltpu.VMEM((width, 1024), BF16),
            pltpu.VMEM((TOK, TOK), F32),
            pltpu.VMEM((2, 2, 3 * TOK, HEAD), BF16),
            pltpu.VMEM((2, 2, 2 * QT, HEAD), BF16),
            pltpu.VMEM((2, 2, 2 * QT, HEAD), BF16),
            pltpu.VMEM((2, 1, 2 * QT), jnp.int32),
            pltpu.VMEM((KEYS, 2 * QT), F32),
            pltpu.VMEM((KEYS, 2 * QT), F32),
            pltpu.VMEM((KEYS, 2 * QT), BF16),
            pltpu.VMEM((KEYS, 2 * QT), BF16),
            pltpu.VMEM((2, 2, 3 * TOK, HEAD), F32),
            pltpu.VMEM((2, 2, 2 * TOK, HEAD), BF16),
            pltpu.VMEM((2, 2, 2, TOK, HEAD), BF16),
            pltpu.VMEM((TOK, 1024), BF16),
            pltpu.VMEM((ncn, 256, nc), BF16),
            pltpu.VMEM((ncn, 256, nc), BF16),
            pltpu.VMEM((ncn, 128, nc), BF16),
            pltpu.VMEM((ncn, 128, nc), BF16),
            pltpu.VMEM((ncn, 128, nc), F32),
            pltpu.VMEM((ncn, 128, nc), F32),
            dma((kcn,)), dma((kcn,)), dma((kcn,)), dma((kcn,)), dma((8,)), dma((ncn,)),
            dma((2, 2)), dma((2, 2)), dma((2, 2)), dma((2, 2)),
            dma((ncn,)), dma((ncn,)), dma((ncn,)), dma((ncn,)),
        ],
        compiler_params=pltpu.CompilerParams(
            collective_id=0, has_side_effects=True, vmem_limit_bytes=60 * 1024 * 1024
        ),
    )(hidden, w_query, key_weight, value_weight, out_gradient, doc_start)


def solution(mesh):
    in_specs = (
        P("ctx", None),
        P(None, "head"),
        P(None, "head"),
        P(None, "head"),
        P("ctx", "head"),
        P("ctx"),
    )
    out_specs = P(("ctx", "head"), None)
    return jax.shard_map(
        functools.partial(shards, n_ctx=mesh.shape["ctx"]),
        mesh=mesh, in_specs=in_specs, out_specs=out_specs, check_vma=False,
    )
```

time: 281 us -> 94.3 us (0.34)
  the two profiles are of different devices: /device:TPU:95 before, /device:TPU:1 now
where the time goes in v1:
time: 94.3 us; the launch traced here: 94.2 us
  Pallas kernels  90.7 us (96%)
  local copies, waits for them, and re-layouts  3.49 us (4%)
    pallas_call x1, Pallas kernels, shards(): pl.pallas_call(functools.partial(kernel, n_ctx, kcn, kc, ncn, nc), out_sh...  90.7 us
    unnamed x1, local copies, waits for them, and re-layouts  3.49 us

profile of v1, /device:TPU:1, one launch (start us, length us, event | category | flops | bytes accessed | tf_op | source)
XLA Modules:
  0.0 94.2 jit_solution(16107278096952571488)
XLA Ops:
  0.0 90.7 %shard_map.64 = f32[128,5376]{1,0:T(8,128)} custom-call(bf16[512,5376]{1,0:T(8,128)(2,1)} %hid.1, bf16[5376,512]{1,0:T(8,128)(2,1)} %wq.1, bf16[5376,256]{1,0:T(8,128)(2,1)} %wk.1, bf16[5376,256]{1,0:T(8,128)(2,1)} %wv.1, bf16[512,512]{1,0:T(8,128)(2,1)} %dog.1, s32[512]{0:T(512)} %doc.1), custom_call_target="tpu_custom_call" | custom-call | tf_op jit(solution)/shard_map/pallas_call | solution.py:298
  90.7 3.5 %copy.8 = f32[128,5376]{1,0:T(8,128)} copy(f32[128,5376]{1,0:T(8,128)} %shard_map.64) | data formatting | bytes 5505024

commit v2 on v1

v2 whole, which is shorter than its diff:
```python
import functools
import math

import jax
import jax.numpy as jnp
from jax import lax
from jax.experimental import pallas as pl
from jax.experimental.pallas import tpu as pltpu
from jax.sharding import PartitionSpec as P

HEAD = 128
WINDOW = 1024
SCALE = 168.0 ** (-0.5)
LOG2E = math.log2(math.e)
MESH = pl.DeviceIdType.MESH
F32 = jnp.float32
BF16 = jnp.bfloat16

TOK = 512
QT = 256
KEYS = 1280
CH = 256
NT = (((1,), (1,)), ((), ()))
TN = (((0,), (0,)), ((), ()))


def kernel(
    n_ctx, kcn, kc, ncn, nc,
    hid, wq, wk, wv, dog, doc, out, rs2_in,
    h, wall, acc, kv, q, do, lo, s, dp, pw, ds, dkv, dkv_out, dkv_in, grad,
    rs1_out, rs1_in, rs2_out, other, keep,
    sem_h, sem_k, sem_v, sem_q, sem_do, sem_o,
    kv_ss, kv_rs, dkv_ss, dkv_rs, r1_ss, r1_rs, r2_ss, r2_rs,
):
    ctx = lax.axis_index("ctx")
    head = lax.axis_index("head")
    zpos, core = head // 2, lax.rem(head, 2)

    def at_ctx(by):
        return (lax.rem(ctx + by + n_ctx, n_ctx), head)

    next1, next2, prev1, prev2 = at_ctx(1), at_ctx(2), at_ctx(-1), at_ctx(-2)
    mate = (ctx, head + 1 - 2 * core)
    across = (ctx, lax.rem(head + 2, 4))

    barrier = pltpu.get_barrier_semaphore()
    for peer in (next1, next2, prev1, prev2, mate, across):
        pl.semaphore_signal(barrier, inc=1, device_id=peer, device_id_type=MESH)

    def cols(k):
        return pl.ds(pl.multiple_of(k * kc, 128), kc)

    def in_h(k):
        return pltpu.make_async_copy(hid.at[:, cols(k)], h.at[k], sem_h.at[k])

    def in_k(g, k):
        return pltpu.make_async_copy(
            wk.at[cols(k), pl.ds(g * HEAD, HEAD)],
            wall.at[cols(k), pl.ds(512 + 256 * g, HEAD)],
            sem_k.at[g, k],
        )

    def in_v(g, k):
        return pltpu.make_async_copy(
            wv.at[cols(k), pl.ds(g * HEAD, HEAD)],
            wall.at[cols(k), pl.ds(512 + 256 * g + HEAD, HEAD)],
            sem_v.at[g, k],
        )

    def in_q(k):
        return pltpu.make_async_copy(wq.at[cols(k), :], wall.at[cols(k), pl.ds(0, 512)], sem_q.at[k])

    for k in range(kcn):
        in_h(k).start()
        in_k(0, k).start()
        in_v(0, k).start()
    for k in range(kcn):
        in_k(1, k).start()
        in_v(1, k).start()
    for k in range(kcn):
        in_q(k).start()
    do_copies = []
    for g in range(2):
        for t in range(2):
            for m in range(2):
                do_copies.append(
                    pltpu.make_async_copy(
                        dog.at[pl.ds(t * QT, QT), pl.ds((2 * g + m) * HEAD, HEAD)],
                        do.at[g, t, pl.ds(m * QT, QT), :],
                        sem_do.at[4 * g + 2 * t + m],
                    )
                )
    for copy in do_copies:
        copy.start()

    first = ctx * TOK
    lane = lax.broadcasted_iota(jnp.int32, (1, TOK), 1)
    low = jnp.maximum(doc[...].reshape(1, TOK) - first + WINDOW, lane + 1)
    for t in range(2):
        part = low[:, t * QT : (t + 1) * QT] - t * QT
        lo[t] = jnp.concatenate([part, part], axis=1)

    def send_kv(g, far):
        return pltpu.make_async_remote_copy(
            src_ref=kv.at[g, :, pl.ds(2 * TOK, TOK), :],
            dst_ref=kv.at[g, :, pl.ds((1 - far) * TOK, TOK), :],
            send_sem=kv_ss.at[g, far],
            recv_sem=kv_rs.at[g, far],
            device_id=next2 if far else next1,
            device_id_type=MESH,
        )

    for g in range(2):
        acc[:, pl.ds(0, 256)] = jnp.zeros((TOK, 256), F32)

        @pl.loop(0, kcn)
        def _(k):
            if g == 0:
                in_h(k).wait()
            in_k(g, k).wait()
            in_v(g, k).wait()
            acc[:, pl.ds(0, 256)] += jnp.dot(
                h[k], wall[cols(k), pl.ds(512 + 256 * g, 256)], preferred_element_type=F32
            )

        for j in range(2):
            kv[g, j, pl.ds(2 * TOK, TOK), :] = acc[:, pl.ds(j * HEAD, HEAD)].astype(BF16)
        if g == 0:
            pl.semaphore_wait(barrier, 6)
        for far in range(2):
            send_kv(g, far).start()

    acc[...] = jnp.zeros_like(acc)

    @pl.loop(0, kcn)
    def _(k):
        in_q(k).wait()
        acc[...] += jnp.dot(h[k], wall[cols(k), pl.ds(0, 512)], preferred_element_type=F32)

    for g in range(2):
        for t in range(2):
            for m in range(2):
                q[g, t, pl.ds(m * QT, QT), :] = acc[
                    pl.ds(t * QT, QT), pl.ds((2 * g + m) * HEAD, HEAD)
                ].astype(BF16)
    for copy in do_copies:
        copy.wait()

    def same(a, b):
        return 1 - (a + b - 2 * a * b)

    def place(b):
        return pl.multiple_of(128 * (2 * same(lax.rem(b, 2), core) + same(b // 2, zpos)), 128)

    def send_dkv(g, far):
        return pltpu.make_async_remote_copy(
            src_ref=dkv_out.at[g, :, pl.ds((1 - far) * TOK, TOK), :],
            dst_ref=dkv_in.at[far, g],
            send_sem=dkv_ss.at[g, far],
            recv_sem=dkv_rs.at[g, far],
            device_id=prev2 if far else prev1,
            device_id_type=MESH,
        )

    @pl.loop(0, 2)
    def _(g):
        for far in range(2):
            send_kv(g, far).wait_recv()
        for t in range(2):
            lowest = lo[t]
            local = lax.broadcasted_iota(jnp.int32, (CH, 2 * QT), 0)

            def chunk(c):
                return pl.ds(c * CH, CH)

            def keys(j, c):
                return kv[g, j, pl.ds((t + c) * CH, CH), :]

            top = None
            for c in range(5):
                kept = lax.dot_general(keys(0, c), q[g, t], NT, preferred_element_type=F32)
                allowed = local >= lowest - c * CH
                if c == 4:
                    lane2 = lax.broadcasted_iota(jnp.int32, (1, QT), 1)
                    allowed = allowed & (local <= jnp.concatenate([lane2, lane2], axis=1))
                kept = jnp.where(allowed, kept, -jnp.inf)
                s[chunk(c), :] = kept
                here = jnp.max(kept, axis=0, keepdims=True)
                top = here if top is None else jnp.maximum(top, here)

            total, dots = 0.0, 0.0
            for c in range(5):
                grads = lax.dot_general(keys(1, c), do[g, t], NT, preferred_element_type=F32)
                weight = jnp.exp2((s[chunk(c), :] - top) * (SCALE * LOG2E))
                s[chunk(c), :] = weight
                dp[chunk(c), :] = grads
                total = total + jnp.sum(weight, axis=0, keepdims=True)
                dots = dots + jnp.sum(weight * grads, axis=0, keepdims=True)
            inverse = 1.0 / total
            row_dot = dots * inverse

            for c in range(5):
                prob = s[chunk(c), :] * inverse
                low_prob = prob.astype(BF16)
                d_score = (prob * (dp[chunk(c), :] - row_dot)).astype(BF16)
                ds[g, t, chunk(c), :] = d_score
                if t + c < 4:
                    rows = pl.ds((t + c) * CH, CH)
                    d_key = jnp.dot(d_score, q[g, t], preferred_element_type=F32)
                    d_val = jnp.dot(low_prob, do[g, t], preferred_element_type=F32)
                    if t == 1:
                        d_key = d_key + dkv[g, 0, rows, :]
                        d_val = d_val + dkv[g, 1, rows, :]
                    if t == 1 or c == 0:
                        dkv_out[g, 0, rows, :] = (d_key * SCALE).astype(BF16)
                        dkv_out[g, 1, rows, :] = d_val.astype(BF16)
                    else:
                        dkv[g, 0, rows, :] = d_key
                        dkv[g, 1, rows, :] = d_val
                else:
                    pw[g, c - 4 if t == 0 else c - 2] = low_prob

        for far in range(2):
            send_dkv(g, far).start()

    @pl.loop(0, 2)
    def _(g):
        for t in range(2):
            dq = lax.dot_general(
                kv[g, 0, pl.ds(t * QT, KEYS), :], ds[g, t], TN, preferred_element_type=F32
            )
            dq = jnp.transpose(dq * SCALE).astype(BF16)
            for m in range(2):
                feats = pl.ds(pl.multiple_of((2 * g + m) * HEAD, HEAD), HEAD)
                for j in range(2):
                    grad[pl.ds(place(2 * t + j), 128), feats] = dq[
                        m * QT + j * 128 : m * QT + (j + 1) * 128
                    ]

        def own(j, first_low, second_low, third_low, by):
            dkv[g, j, pl.ds(4 * CH, CH), :] = jnp.dot(
                first_low, by[g, 0], preferred_element_type=F32
            ) + jnp.dot(second_low, by[g, 1], preferred_element_type=F32)
            dkv[g, j, pl.ds(5 * CH, CH), :] = jnp.dot(third_low, by[g, 1], preferred_element_type=F32)

        last = pl.ds(4 * CH, CH)
        own(0, ds[g, 0, last, :], ds[g, 1, pl.ds(3 * CH, CH), :], ds[g, 1, last, :], q)
        own(1, pw[g, 0], pw[g, 1], pw[g, 2], do)

    for g in range(2):
        for far in range(2):
            send_dkv(g, far).wait_recv()
        for j in range(2):
            for b in range(4):
                rows = pl.ds(b * 128, 128)
                own = dkv[g, j, pl.ds(2 * TOK + b * 128, 128), :]
                if j == 0:
                    own = own * SCALE
                whole = own + (dkv_in[0, g, j, rows, :].astype(F32) + dkv_in[1, g, j, rows, :].astype(F32))
                grad[pl.ds(place(b), 128), pl.ds(512 + g * 256 + j * HEAD, HEAD)] = whole.astype(BF16)

    def send_r1(c):
        return pltpu.make_async_remote_copy(
            src_ref=rs1_out.at[c], dst_ref=rs1_in.at[c],
            send_sem=r1_ss.at[c], recv_sem=r1_rs.at[c],
            device_id=mate, device_id_type=MESH,
        )

    def out_cols(c):
        return pl.ds(pl.multiple_of(c * nc, nc), nc)

    def send_r2(c):
        return pltpu.make_async_remote_copy(
            src_ref=rs2_out.at[c], dst_ref=rs2_in.at[:, out_cols(c)],
            send_sem=r2_ss.at[c], recv_sem=r2_rs.at[c],
            device_id=across, device_id_type=MESH,
        )

    def out_copy(c):
        return pltpu.make_async_copy(keep.at[c], out.at[:, out_cols(c)], sem_o.at[c])

    def join(c):
        send_r1(c).wait_recv()
        rs2_out[c] = (other[c] + rs1_in[c, pl.ds(0, 128), :].astype(F32)).astype(BF16)
        send_r2(c).start()
        keep[c] = keep[c] + rs1_in[c, pl.ds(128, 128), :].astype(F32)
        out_copy(c).start()

    @pl.loop(0, ncn)
    def _(c):
        part = lax.dot_general(
            grad[...], wall[pl.ds(pl.multiple_of(c * nc, nc), nc), :], NT, preferred_element_type=F32
        )
        rs1_out[c] = part[:256].astype(BF16)
        other[c] = part[256:384]
        keep[c] = part[384:]
        send_r1(c).start()

        @pl.when(c > 0)
        def _():
            join(c - 1)

    join(ncn - 1)

    @pl.loop(0, ncn)
    def _(c):
        out_copy(c).wait()
        send_r1(c).wait_send()
        send_r2(c).wait_send()
        send_r2(c).wait_recv()

    for g in range(2):
        for far in range(2):
            send_kv(g, far).wait_send()
            send_dkv(g, far).wait_send()


def shards(hidden, w_query, key_weight, value_weight, out_gradient, doc_start, *, n_ctx):
    width = hidden.shape[1]
    kcn = 7
    kc = width // kcn
    nc = 256
    ncn = width // nc
    dma = pltpu.SemaphoreType.DMA
    anywhere = pl.BlockSpec(memory_space=pl.ANY)
    own, across = pl.pallas_call(
        functools.partial(kernel, n_ctx, kcn, kc, ncn, nc),
        out_shape=(
            jax.ShapeDtypeStruct((128, width), F32),
            jax.ShapeDtypeStruct((128, width), BF16),
        ),
        in_specs=[anywhere] * 5 + [pl.BlockSpec(memory_space=pltpu.VMEM)],
        out_specs=(anywhere, anywhere),
        scratch_shapes=[
            pltpu.VMEM((kcn, TOK, kc), BF16),
            pltpu.VMEM((width, 1024), BF16),
            pltpu.VMEM((TOK, TOK), F32),
            pltpu.VMEM((2, 2, 3 * TOK, HEAD), BF16),
            pltpu.VMEM((2, 2, 2 * QT, HEAD), BF16),
            pltpu.VMEM((2, 2, 2 * QT, HEAD), BF16),
            pltpu.VMEM((2, 1, 2 * QT), jnp.int32),
            pltpu.VMEM((KEYS, 2 * QT), F32),
            pltpu.VMEM((KEYS, 2 * QT), F32),
            pltpu.VMEM((2, 3, CH, 2 * QT), BF16),
            pltpu.VMEM((2, 2, KEYS, 2 * QT), BF16),
            pltpu.VMEM((2, 2, 3 * TOK, HEAD), F32),
            pltpu.VMEM((2, 2, 2 * TOK, HEAD), BF16),
            pltpu.VMEM((2, 2, 2, TOK, HEAD), BF16),
            pltpu.VMEM((TOK, 1024), BF16),
            pltpu.VMEM((ncn, 256, nc), BF16),
            pltpu.VMEM((ncn, 256, nc), BF16),
            pltpu.VMEM((ncn, 128, nc), BF16),
            pltpu.VMEM((ncn, 128, nc), F32),
            pltpu.VMEM((ncn, 128, nc), F32),
            dma((kcn,)), dma((2, kcn)), dma((2, kcn)), dma((kcn,)), dma((8,)), dma((ncn,)),
            dma((2, 2)), dma((2, 2)), dma((2, 2)), dma((2, 2)),
            dma((ncn,)), dma((ncn,)), dma((ncn,)), dma((ncn,)),
        ],
        compiler_params=pltpu.CompilerParams(
            collective_id=0, has_side_effects=True, vmem_limit_bytes=60 * 1024 * 1024
        ),
    )(hidden, w_query, key_weight, value_weight, out_gradient, doc_start)
    return own + across.astype(F32)


def solution(mesh):
    in_specs = (
        P("ctx", None),
        P(None, "head"),
        P(None, "head"),
        P(None, "head"),
        P("ctx", "head"),
        P("ctx"),
    )
    out_specs = P(("ctx", "head"), None)
    return jax.shard_map(
        functools.partial(shards, n_ctx=mesh.shape["ctx"]),
        mesh=mesh, in_specs=in_specs, out_specs=out_specs, check_vma=False,
    )
```

time: 94.3 us -> 89.7 us (0.951)
  Pallas kernels: 90.7 us -> 85.6 us
  other arithmetic: 0 us -> 3.93 us
  local copies, waits for them, and re-layouts: 3.49 us -> 0 us
    pallas_call x1, Pallas kernels: 90.7 us -> 85.6 us  [shards(): pl.pallas_call(functools.partial(kernel, n_ctx, kcn, kc, ncn, nc), out_sh...]
    add x0 -> x1, other arithmetic: none -> 3.93 us  [shards(): return own + across.astype(F32)]
    unnamed x1 -> x0, local copies, waits for them, and re-layouts: 3.49 us -> none
where the time goes in v2:
time: 89.7 us; the launch traced here: 89.5 us
  Pallas kernels  85.6 us (95%)
  other arithmetic  3.93 us (4%)
    pallas_call x1, Pallas kernels, shards(): pl.pallas_call(functools.partial(kernel, n_ctx, kcn, kc, ncn, nc), out_sh...  85.6 us
    add x1, other arithmetic, shards(): return own + across.astype(F32)  3.93 us

profile of v2, /device:TPU:1, one launch (start us, length us, event | category | flops | bytes accessed | tf_op | source)
XLA Modules:
  0.0 89.5 jit_solution(558040043185173680)
XLA Ops:
  0.0 85.6 %shard_map.64 = (f32[128,5376]{1,0:T(8,128)}, bf16[128,5376]{1,0:T(8,128)(2,1)}) custom-call(bf16[512,5376]{1,0:T(8,128)(2,1)} %hid.1, bf16[5376,512]{1,0:T(8,128)(2,1)} %wq.1, bf16[5376,256]{1,0:T(8,128)(2,1)} %wk.1, bf16[5376,256]{1,0:T(8,128)(2,1)} %wv.1, bf16[512,512]{1,0:T(8,128)(2,1)} %dog.1, s32[512]{0:T(512)} %doc.1), custom_call_target="tpu_custom_call" | custom-call | tf_op jit(solution)/shard_map/pallas_call | solution.py:326
  85.6 3.9 %convert_add_fusion = f32[128,5376]{1,0:T(8,128)} fusion(f32[128,5376]{1,0:T(8,128)} %get-tuple-element.7, bf16[128,5376]{1,0:T(8,128)(2,1)} %get-tuple-element.8), kind=kLoop, calls=%fused_computation | loop fusion | flops 1376256 | bytes 6881280 | tf_op jit(solution)/shard_map/add | solution.py:363

commit v3 on v2

--- a/solution.py
+++ b/solution.py
@@ -39,12 +39,14 @@
     def at_ctx(by):
         return (lax.rem(ctx + by + n_ctx, n_ctx), head)
 
-    next1, next2, prev1, prev2 = at_ctx(1), at_ctx(2), at_ctx(-1), at_ctx(-2)
+    next2, prev2 = at_ctx(2), at_ctx(-2)
+    odd = lax.rem(ctx, 2)
+    pair = (ctx + 1 - 2 * odd, head)
     mate = (ctx, head + 1 - 2 * core)
     across = (ctx, lax.rem(head + 2, 4))
 
     barrier = pltpu.get_barrier_semaphore()
-    for peer in (next1, next2, prev1, prev2, mate, across):
+    for peer in (next2, prev2, pair, mate, across):
         pl.semaphore_signal(barrier, inc=1, device_id=peer, device_id_type=MESH)
 
     def cols(k):
@@ -100,15 +102,23 @@
         part = low[:, t * QT : (t + 1) * QT] - t * QT
         lo[t] = jnp.concatenate([part, part], axis=1)
 
-    def send_kv(g, far):
+    def send_kv(g, j, far):
+        if far:
+            source, rows, device = 2 * TOK, 0, next2
+        else:
+            source, rows, device = pl.multiple_of(2 * TOK * (1 - odd), TOK), TOK, pair
         return pltpu.make_async_remote_copy(
-            src_ref=kv.at[g, :, pl.ds(2 * TOK, TOK), :],
-            dst_ref=kv.at[g, :, pl.ds((1 - far) * TOK, TOK), :],
-            send_sem=kv_ss.at[g, far],
-            recv_sem=kv_rs.at[g, far],
-            device_id=next2 if far else next1,
+            src_ref=kv.at[g, j, pl.ds(source, TOK), :],
+            dst_ref=kv.at[g, j, pl.ds(rows, TOK), :],
+            send_sem=kv_ss.at[g, j, far],
+            recv_sem=kv_rs.at[g, j, far],
+            device_id=device,
             device_id_type=MESH,
         )
+
+    def relay_kv(g, j):
+        send_kv(g, j, 1).wait_recv()
+        send_kv(g, j, 0).start()
 
     for g in range(2):
         acc[:, pl.ds(0, 256)] = jnp.zeros((TOK, 256), F32)
@@ -126,9 +136,13 @@
         for j in range(2):
             kv[g, j, pl.ds(2 * TOK, TOK), :] = acc[:, pl.ds(j * HEAD, HEAD)].astype(BF16)
         if g == 0:
-            pl.semaphore_wait(barrier, 6)
-        for far in range(2):
-            send_kv(g, far).start()
+            pl.semaphore_wait(barrier, 5)
+        for j in range(2):
+            send_kv(g, j, 1).start()
+
+            @pl.when(odd == 0)
+            def _():
+                send_kv(g, j, 0).start()
 
     acc[...] = jnp.zeros_like(acc)
 
@@ -152,20 +166,38 @@
     def place(b):
         return pl.multiple_of(128 * (2 * same(lax.rem(b, 2), core) + same(b // 2, zpos)), 128)
 
-    def send_dkv(g, far):
+    def send_dkv(g, j, far):
         return pltpu.make_async_remote_copy(
-            src_ref=dkv_out.at[g, :, pl.ds((1 - far) * TOK, TOK), :],
-            dst_ref=dkv_in.at[far, g],
-            send_sem=dkv_ss.at[g, far],
-            recv_sem=dkv_rs.at[g, far],
-            device_id=prev2 if far else prev1,
+            src_ref=dkv_out.at[g, j, pl.ds((1 - far) * TOK, TOK), :],
+            dst_ref=dkv_in.at[far, g, j],
+            send_sem=dkv_ss.at[g, j, far],
+            recv_sem=dkv_rs.at[g, j, far],
+            device_id=prev2 if far else pair,
             device_id_type=MESH,
         )
+
+    def relay_dkv(g, j):
+        send_dkv(g, j, 0).wait_recv()
+        rows = pl.ds(0, TOK)
+        dkv_out[g, j, rows, :] = (
+            dkv_out[g, j, rows, :].astype(F32) + dkv_in[0, g, j].astype(F32)
+        ).astype(BF16)
+        send_dkv(g, j, 1).start()
+
+    @pl.when(odd == 1)
+    def _():
+        for j in range(2):
+            relay_kv(0, j)
 
     @pl.loop(0, 2)
     def _(g):
-        for far in range(2):
-            send_kv(g, far).wait_recv()
+        @pl.when(odd == 0)
+        def _():
+            for j in range(2):
+                send_kv(g, j, 1).wait_recv()
+
+        for j in range(2):
+            send_kv(g, j, 0).wait_recv()
         for t in range(2):
             lowest = lo[t]
             local = lax.broadcasted_iota(jnp.int32, (CH, 2 * QT), 0)
@@ -220,8 +252,21 @@
                 else:
                     pw[g, c - 4 if t == 0 else c - 2] = low_prob
 
-        for far in range(2):
-            send_dkv(g, far).start()
+            @pl.when((odd == 1) & (g == 0))
+            def _():
+                relay_kv(1, t)
+
+        for j in range(2):
+            send_dkv(g, j, 0).start()
+
+            @pl.when(odd == 0)
+            def _():
+                send_dkv(g, j, 1).start()
+
+    @pl.when(odd == 1)
+    def _():
+        for j in range(2):
+            relay_dkv(0, j)
 
     @pl.loop(0, 2)
     def _(g):
@@ -247,16 +292,25 @@
         own(0, ds[g, 0, last, :], ds[g, 1, pl.ds(3 * CH, CH), :], ds[g, 1, last, :], q)
         own(1, pw[g, 0], pw[g, 1], pw[g, 2], do)
 
+    @pl.when(odd == 1)
+    def _():
+        for j in range(2):
+            relay_dkv(1, j)
+
     for g in range(2):
-        for far in range(2):
-            send_dkv(g, far).wait_recv()
-        for j in range(2):
+        for j in range(2):
+            @pl.when(odd == 0)
+            def _():
+                send_dkv(g, j, 0).wait_recv()
+
+            send_dkv(g, j, 1).wait_recv()
             for b in range(4):
                 rows = pl.ds(b * 128, 128)
                 own = dkv[g, j, pl.ds(2 * TOK + b * 128, 128), :]
                 if j == 0:
                     own = own * SCALE
-                whole = own + (dkv_in[0, g, j, rows, :].astype(F32) + dkv_in[1, g, j, rows, :].astype(F32))
+                near = jnp.where(odd == 0, dkv_in[0, g, j, rows, :].astype(F32), 0.0)
+                whole = own + (near + dkv_in[1, g, j, rows, :].astype(F32))
                 grad[pl.ds(place(b), 128), pl.ds(512 + g * 256 + j * HEAD, HEAD)] = whole.astype(BF16)
 
     def send_r1(c):
@@ -310,9 +364,10 @@
         send_r2(c).wait_recv()
 
     for g in range(2):
-        for far in range(2):
-            send_kv(g, far).wait_send()
-            send_dkv(g, far).wait_send()
+        for j in range(2):
+            for far in range(2):
+                send_kv(g, j, far).wait_send()
+                send_dkv(g, j, far).wait_send()
 
 
 def shards(hidden, w_query, key_weight, value_weight, out_gradient, doc_start, *, n_ctx):
@@ -353,7 +408,7 @@
             pltpu.VMEM((ncn, 128, nc), F32),
             pltpu.VMEM((ncn, 128, nc), F32),
             dma((kcn,)), dma((2, kcn)), dma((2, kcn)), dma((kcn,)), dma((8,)), dma((ncn,)),
-            dma((2, 2)), dma((2, 2)), dma((2, 2)), dma((2, 2)),
+            dma((2, 2, 2)), dma((2, 2, 2)), dma((2, 2, 2)), dma((2, 2, 2)),
             dma((ncn,)), dma((ncn,)), dma((ncn,)), dma((ncn,)),
         ],
         compiler_params=pltpu.CompilerParams(

time: 89.7 us -> 84.4 us (0.941)
  the two profiles are of different devices: /device:TPU:1 before, /device:TPU:95 now
where the time goes in v3:
time: 84.4 us; the launch traced here: 84.3 us
  Pallas kernels  80.4 us (95%)
  other arithmetic  3.93 us (5%)
    pallas_call x1, Pallas kernels, shards(): pl.pallas_call(functools.partial(kernel, n_ctx, kcn, kc, ncn, nc), out_sh...  80.4 us
    add x1, other arithmetic, shards(): return own + across.astype(F32)  3.93 us

profile of v3, /device:TPU:95, one launch (start us, length us, event | category | flops | bytes accessed | tf_op | source)
XLA Modules:
  0.0 84.3 jit_solution(12836986322436595726)
XLA Ops:
  0.0 80.4 %shard_map.64 = (f32[128,5376]{1,0:T(8,128)}, bf16[128,5376]{1,0:T(8,128)(2,1)}) custom-call(bf16[512,5376]{1,0:T(8,128)(2,1)} %hid.1, bf16[5376,512]{1,0:T(8,128)(2,1)} %wq.1, bf16[5376,256]{1,0:T(8,128)(2,1)} %wk.1, bf16[5376,256]{1,0:T(8,128)(2,1)} %wv.1, bf16[512,512]{1,0:T(8,128)(2,1)} %dog.1, s32[512]{0:T(512)} %doc.1), custom_call_target="tpu_custom_call" | custom-call | tf_op jit(solution)/shard_map/pallas_call | solution.py:381
  80.4 3.9 %convert_add_fusion = f32[128,5376]{1,0:T(8,128)} fusion(f32[128,5376]{1,0:T(8,128)} %get-tuple-element.7, bf16[128,5376]{1,0:T(8,128)(2,1)} %get-tuple-element.8), kind=kLoop, calls=%fused_computation | loop fusion | flops 1376256 | bytes 6881280 | tf_op jit(solution)/shard_map/add | solution.py:418

commit v4 on v3

--- a/solution.py
+++ b/solution.py
@@ -26,10 +26,10 @@
 
 def kernel(
     n_ctx, kcn, kc, ncn, nc,
-    hid, wq, wk, wv, dog, doc, out, rs2_in,
+    hid, wq, wk, wv, dog, doc, keep, rs2_in,
     h, wall, acc, kv, q, do, lo, s, dp, pw, ds, dkv, dkv_out, dkv_in, grad,
-    rs1_out, rs1_in, rs2_out, other, keep,
-    sem_h, sem_k, sem_v, sem_q, sem_do, sem_o,
+    rs1_out, rs1_in, rs2_out, other,
+    sem_h, sem_k, sem_v, sem_q, sem_do,
     kv_ss, kv_rs, dkv_ss, dkv_rs, r1_ss, r1_rs, r2_ss, r2_rs,
 ):
     ctx = lax.axis_index("ctx")
@@ -330,15 +330,11 @@
             device_id=across, device_id_type=MESH,
         )
 
-    def out_copy(c):
-        return pltpu.make_async_copy(keep.at[c], out.at[:, out_cols(c)], sem_o.at[c])
-
     def join(c):
         send_r1(c).wait_recv()
         rs2_out[c] = (other[c] + rs1_in[c, pl.ds(0, 128), :].astype(F32)).astype(BF16)
         send_r2(c).start()
-        keep[c] = keep[c] + rs1_in[c, pl.ds(128, 128), :].astype(F32)
-        out_copy(c).start()
+        keep[:, out_cols(c)] += rs1_in[c, pl.ds(128, 128), :].astype(F32)
 
     @pl.loop(0, ncn)
     def _(c):
@@ -347,7 +343,7 @@
         )
         rs1_out[c] = part[:256].astype(BF16)
         other[c] = part[256:384]
-        keep[c] = part[384:]
+        keep[:, out_cols(c)] = part[384:]
         send_r1(c).start()
 
         @pl.when(c > 0)
@@ -358,7 +354,6 @@
 
     @pl.loop(0, ncn)
     def _(c):
-        out_copy(c).wait()
         send_r1(c).wait_send()
         send_r2(c).wait_send()
         send_r2(c).wait_recv()
@@ -381,11 +376,11 @@
     own, across = pl.pallas_call(
         functools.partial(kernel, n_ctx, kcn, kc, ncn, nc),
         out_shape=(
-            jax.ShapeDtypeStruct((128, width), F32),
-            jax.ShapeDtypeStruct((128, width), BF16),
+            pltpu.VMEM((128, width), F32),
+            pltpu.VMEM((128, width), BF16),
         ),
         in_specs=[anywhere] * 5 + [pl.BlockSpec(memory_space=pltpu.VMEM)],
-        out_specs=(anywhere, anywhere),
+        out_specs=(pl.BlockSpec(memory_space=pltpu.VMEM),) * 2,
         scratch_shapes=[
             pltpu.VMEM((kcn, TOK, kc), BF16),
             pltpu.VMEM((width, 1024), BF16),
@@ -406,8 +401,7 @@
             pltpu.VMEM((ncn, 256, nc), BF16),
             pltpu.VMEM((ncn, 128, nc), BF16),
             pltpu.VMEM((ncn, 128, nc), F32),
-            pltpu.VMEM((ncn, 128, nc), F32),
-            dma((kcn,)), dma((2, kcn)), dma((2, kcn)), dma((kcn,)), dma((8,)), dma((ncn,)),
+            dma((kcn,)), dma((2, kcn)), dma((2, kcn)), dma((kcn,)), dma((8,)),
             dma((2, 2, 2)), dma((2, 2, 2)), dma((2, 2, 2)), dma((2, 2, 2)),
             dma((ncn,)), dma((ncn,)), dma((ncn,)), dma((ncn,)),
         ],

time: 84.4 us -> 82 us (0.972)
  other arithmetic: 3.93 us -> 1.76 us
    add x1, other arithmetic: 3.93 us -> 1.76 us  [shards(): return own + across.astype(F32)]
where the time goes in v4:
time: 82 us; the launch traced here: 81.9 us
  Pallas kernels  80.1 us (98%)
  other arithmetic  1.76 us (2%)
    pallas_call x1, Pallas kernels, shards(): pl.pallas_call(functools.partial(kernel, n_ctx, kcn, kc, ncn, nc), out_sh...  80.1 us
    add x1, other arithmetic, shards(): return own + across.astype(F32)  1.76 us

profile of v4, /device:TPU:95, one launch (start us, length us, event | category | flops | bytes accessed | tf_op | source)
XLA Modules:
  0.0 81.9 jit_solution(14430981327997218360)
XLA Ops:
  0.0 80.1 %shard_map.64 = (f32[128,5376]{1,0:T(8,128)S(1)}, bf16[128,5376]{1,0:T(8,128)(2,1)S(1)}) custom-call(bf16[512,5376]{1,0:T(8,128)(2,1)} %hid.1, bf16[5376,512]{1,0:T(8,128)(2,1)} %wq.1, bf16[5376,256]{1,0:T(8,128)(2,1)} %wk.1, bf16[5376,256]{1,0:T(8,128)(2,1)} %wv.1, bf16[512,512]{1,0:T(8,128)(2,1)} %dog.1, s32[512]{0:T(512)} %doc.1), custom_call_target="tpu_custom_call" | custom-call | tf_op jit(solution)/shard_map/pallas_call | solution.py:376
  80.1 1.8 %convert_add_fusion = f32[128,5376]{1,0:T(8,128)} fusion(f32[128,5376]{1,0:T(8,128)S(1)} %get-tuple-element.7, bf16[128,5376]{1,0:T(8,128)(2,1)S(1)} %get-tuple-element.8), kind=kLoop, calls=%fused_computation | loop fusion | flops 1376256 | bytes 6881280 | tf_op jit(solution)/shard_map/add | solution.py:412

commit v5 on v4

--- a/solution.py
+++ b/solution.py
@@ -102,23 +102,24 @@
         part = low[:, t * QT : (t + 1) * QT] - t * QT
         lo[t] = jnp.concatenate([part, part], axis=1)
 
-    def send_kv(g, j, far):
+    def send_kv(g, j, half, far):
         if far:
             source, rows, device = 2 * TOK, 0, next2
         else:
             source, rows, device = pl.multiple_of(2 * TOK * (1 - odd), TOK), TOK, pair
         return pltpu.make_async_remote_copy(
-            src_ref=kv.at[g, j, pl.ds(source, TOK), :],
-            dst_ref=kv.at[g, j, pl.ds(rows, TOK), :],
-            send_sem=kv_ss.at[g, j, far],
-            recv_sem=kv_rs.at[g, j, far],
+            src_ref=kv.at[g, j, pl.ds(source + half * QT, QT), :],
+            dst_ref=kv.at[g, j, pl.ds(rows + half * QT, QT), :],
+            send_sem=kv_ss.at[g, j, half, far],
+            recv_sem=kv_rs.at[g, j, half, far],
             device_id=device,
             device_id_type=MESH,
         )
 
     def relay_kv(g, j):
-        send_kv(g, j, 1).wait_recv()
-        send_kv(g, j, 0).start()
+        for half in range(2):
+            send_kv(g, j, half, 1).wait_recv()
+            send_kv(g, j, half, 0).start()
 
     for g in range(2):
         acc[:, pl.ds(0, 256)] = jnp.zeros((TOK, 256), F32)
@@ -138,11 +139,12 @@
         if g == 0:
             pl.semaphore_wait(barrier, 5)
         for j in range(2):
-            send_kv(g, j, 1).start()
-
-            @pl.when(odd == 0)
-            def _():
-                send_kv(g, j, 0).start()
+            for half in range(2):
+                send_kv(g, j, half, 1).start()
+
+                @pl.when(odd == 0)
+                def _():
+                    send_kv(g, j, half, 0).start()
 
     acc[...] = jnp.zeros_like(acc)
 
@@ -164,25 +166,24 @@
         return 1 - (a + b - 2 * a * b)
 
     def place(b):
-        return pl.multiple_of(128 * (2 * same(lax.rem(b, 2), core) + same(b // 2, zpos)), 128)
-
-    def send_dkv(g, j, far):
+        return pl.multiple_of(64 * (2 * same(lax.rem(b, 2), core) + same(b // 2, zpos)), 64)
+
+    def send_dkv(g, j, half, far):
         return pltpu.make_async_remote_copy(
-            src_ref=dkv_out.at[g, j, pl.ds((1 - far) * TOK, TOK), :],
-            dst_ref=dkv_in.at[far, g, j],
-            send_sem=dkv_ss.at[g, j, far],
-            recv_sem=dkv_rs.at[g, j, far],
+            src_ref=dkv_out.at[g, j, 1 - far, :, half],
+            dst_ref=dkv_in.at[far, g, j, :, half],
+            send_sem=dkv_ss.at[g, j, half, far],
+            recv_sem=dkv_rs.at[g, j, half, far],
             device_id=prev2 if far else pair,
             device_id_type=MESH,
         )
 
-    def relay_dkv(g, j):
-        send_dkv(g, j, 0).wait_recv()
-        rows = pl.ds(0, TOK)
-        dkv_out[g, j, rows, :] = (
-            dkv_out[g, j, rows, :].astype(F32) + dkv_in[0, g, j].astype(F32)
+    def relay_dkv(g, j, half):
+        send_dkv(g, j, half, 0).wait_recv()
+        dkv_out[g, j, 0, :, half] = (
+            dkv_out[g, j, 0, :, half].astype(F32) + dkv_in[0, g, j, :, half].astype(F32)
         ).astype(BF16)
-        send_dkv(g, j, 1).start()
+        send_dkv(g, j, half, 1).start()
 
     @pl.when(odd == 1)
     def _():
@@ -194,10 +195,12 @@
         @pl.when(odd == 0)
         def _():
             for j in range(2):
-                send_kv(g, j, 1).wait_recv()
+                for half in range(2):
+                    send_kv(g, j, half, 1).wait_recv()
 
         for j in range(2):
-            send_kv(g, j, 0).wait_recv()
+            for half in range(2):
+                send_kv(g, j, half, 0).wait_recv()
         for t in range(2):
             lowest = lo[t]
             local = lax.broadcasted_iota(jnp.int32, (CH, 2 * QT), 0)
@@ -244,8 +247,10 @@
                         d_key = d_key + dkv[g, 0, rows, :]
                         d_val = d_val + dkv[g, 1, rows, :]
                     if t == 1 or c == 0:
-                        dkv_out[g, 0, rows, :] = (d_key * SCALE).astype(BF16)
-                        dkv_out[g, 1, rows, :] = d_val.astype(BF16)
+                        blocks = pl.ds(2 * ((t + c) % 2), 2)
+                        split = (2, 2, 64, HEAD)
+                        dkv_out[g, 0, (t + c) // 2, blocks] = (d_key * SCALE).astype(BF16).reshape(split)
+                        dkv_out[g, 1, (t + c) // 2, blocks] = d_val.astype(BF16).reshape(split)
                     else:
                         dkv[g, 0, rows, :] = d_key
                         dkv[g, 1, rows, :] = d_val
@@ -256,17 +261,13 @@
             def _():
                 relay_kv(1, t)
 
-        for j in range(2):
-            send_dkv(g, j, 0).start()
-
-            @pl.when(odd == 0)
-            def _():
-                send_dkv(g, j, 1).start()
-
-    @pl.when(odd == 1)
-    def _():
-        for j in range(2):
-            relay_dkv(0, j)
+        for half in range(2):
+            for j in range(2):
+                send_dkv(g, j, half, 0).start()
+
+                @pl.when(odd == 0)
+                def _():
+                    send_dkv(g, j, half, 1).start()
 
     @pl.loop(0, 2)
     def _(g):
@@ -278,9 +279,9 @@
             for m in range(2):
                 feats = pl.ds(pl.multiple_of((2 * g + m) * HEAD, HEAD), HEAD)
                 for j in range(2):
-                    grad[pl.ds(place(2 * t + j), 128), feats] = dq[
-                        m * QT + j * 128 : m * QT + (j + 1) * 128
-                    ]
+                    for half in range(2):
+                        start = m * QT + j * 128 + half * 64
+                        grad[half, pl.ds(place(2 * t + j), 64), feats] = dq[start : start + 64]
 
         def own(j, first_low, second_low, third_low, by):
             dkv[g, j, pl.ds(4 * CH, CH), :] = jnp.dot(
@@ -294,75 +295,84 @@
 
     @pl.when(odd == 1)
     def _():
-        for j in range(2):
-            relay_dkv(1, j)
+        for g in range(2):
+            for half in range(2):
+                for j in range(2):
+                    relay_dkv(g, j, half)
+
+    def send_r1(half, c):
+        return pltpu.make_async_remote_copy(
+            src_ref=rs1_out.at[half, c], dst_ref=rs1_in.at[half, c],
+            send_sem=r1_ss.at[half, c], recv_sem=r1_rs.at[half, c],
+            device_id=mate, device_id_type=MESH,
+        )
+
+    def out_cols(c):
+        return pl.ds(pl.multiple_of(c * nc, nc), nc)
+
+    def out_rows(half):
+        return pl.ds(pl.multiple_of(half * 64, 64), 64)
+
+    def send_r2(half, c):
+        return pltpu.make_async_remote_copy(
+            src_ref=rs2_out.at[half, c], dst_ref=rs2_in.at[out_rows(half), out_cols(c)],
+            send_sem=r2_ss.at[half, c], recv_sem=r2_rs.at[half, c],
+            device_id=across, device_id_type=MESH,
+        )
+
+    def join(half, c):
+        send_r1(half, c).wait_recv()
+        rs2_out[half, c] = (other[c] + rs1_in[half, c, pl.ds(0, 64), :].astype(F32)).astype(BF16)
+        send_r2(half, c).start()
+        keep[out_rows(half), out_cols(c)] += rs1_in[half, c, pl.ds(64, 64), :].astype(F32)
+
+    @pl.loop(0, 2)
+    def _(half):
+        for g in range(2):
+            for j in range(2):
+                @pl.when(odd == 0)
+                def _():
+                    send_dkv(g, j, half, 0).wait_recv()
+
+                send_dkv(g, j, half, 1).wait_recv()
+                for b in range(4):
+                    own = dkv[g, j, pl.ds(pl.multiple_of(2 * TOK + b * 128 + half * 64, 64), 64), :]
+                    if j == 0:
+                        own = own * SCALE
+                    near = jnp.where(odd == 0, dkv_in[0, g, j, b, half].astype(F32), 0.0)
+                    whole = own + (near + dkv_in[1, g, j, b, half].astype(F32))
+                    grad[half, pl.ds(place(b), 64), pl.ds(512 + g * 256 + j * HEAD, HEAD)] = whole.astype(BF16)
+
+        @pl.loop(0, ncn)
+        def _(c):
+            part = lax.dot_general(
+                grad[half], wall[out_cols(c), :], NT, preferred_element_type=F32
+            )
+            rs1_out[half, c] = part[:128].astype(BF16)
+            send_r1(half, c).start()
+
+            @pl.when(c > 0)
+            def _():
+                join(half, c - 1)
+
+            other[c] = part[128:192]
+            keep[out_rows(half), out_cols(c)] = part[192:]
+
+        join(half, ncn - 1)
+
+    @pl.loop(0, ncn)
+    def _(c):
+        for half in range(2):
+            send_r1(half, c).wait_send()
+            send_r2(half, c).wait_send()
+            send_r2(half, c).wait_recv()
 
     for g in range(2):
         for j in range(2):
-            @pl.when(odd == 0)
-            def _():
-                send_dkv(g, j, 0).wait_recv()
-
-            send_dkv(g, j, 1).wait_recv()
-            for b in range(4):
-                rows = pl.ds(b * 128, 128)
-                own = dkv[g, j, pl.ds(2 * TOK + b * 128, 128), :]
-                if j == 0:
-                    own = own * SCALE
-                near = jnp.where(odd == 0, dkv_in[0, g, j, rows, :].astype(F32), 0.0)
-                whole = own + (near + dkv_in[1, g, j, rows, :].astype(F32))
-                grad[pl.ds(place(b), 128), pl.ds(512 + g * 256 + j * HEAD, HEAD)] = whole.astype(BF16)
-
-    def send_r1(c):
-        return pltpu.make_async_remote_copy(
-            src_ref=rs1_out.at[c], dst_ref=rs1_in.at[c],
-            send_sem=r1_ss.at[c], recv_sem=r1_rs.at[c],
-            device_id=mate, device_id_type=MESH,
-        )
-
-    def out_cols(c):
-        return pl.ds(pl.multiple_of(c * nc, nc), nc)
-
-    def send_r2(c):
-        return pltpu.make_async_remote_copy(
-            src_ref=rs2_out.at[c], dst_ref=rs2_in.at[:, out_cols(c)],
-            send_sem=r2_ss.at[c], recv_sem=r2_rs.at[c],
-            device_id=across, device_id_type=MESH,
-        )
-
-    def join(c):
-        send_r1(c).wait_recv()
-        rs2_out[c] = (other[c] + rs1_in[c, pl.ds(0, 128), :].astype(F32)).astype(BF16)
-        send_r2(c).start()
-        keep[:, out_cols(c)] += rs1_in[c, pl.ds(128, 128), :].astype(F32)
-
-    @pl.loop(0, ncn)
-    def _(c):
-        part = lax.dot_general(
-            grad[...], wall[pl.ds(pl.multiple_of(c * nc, nc), nc), :], NT, preferred_element_type=F32
-        )
-        rs1_out[c] = part[:256].astype(BF16)
-        other[c] = part[256:384]
-        keep[:, out_cols(c)] = part[384:]
-        send_r1(c).start()
-
-        @pl.when(c > 0)
-        def _():
-            join(c - 1)
-
-    join(ncn - 1)
-
-    @pl.loop(0, ncn)
-    def _(c):
-        send_r1(c).wait_send()
-        send_r2(c).wait_send()
-        send_r2(c).wait_recv()
-
-    for g in range(2):
-        for j in range(2):
-            for far in range(2):
-                send_kv(g, j, far).wait_send()
-                send_dkv(g, j, far).wait_send()
+            for half in range(2):
+                for far in range(2):
+                    send_kv(g, j, half, far).wait_send()
+                    send_dkv(g, j, half, far).wait_send()
 
 
 def shards(hidden, w_query, key_weight, value_weight, out_gradient, doc_start, *, n_ctx):
@@ -394,16 +404,16 @@
             pltpu.VMEM((2, 3, CH, 2 * QT), BF16),
             pltpu.VMEM((2, 2, KEYS, 2 * QT), BF16),
             pltpu.VMEM((2, 2, 3 * TOK, HEAD), F32),
-            pltpu.VMEM((2, 2, 2 * TOK, HEAD), BF16),
-            pltpu.VMEM((2, 2, 2, TOK, HEAD), BF16),
-            pltpu.VMEM((TOK, 1024), BF16),
-            pltpu.VMEM((ncn, 256, nc), BF16),
-            pltpu.VMEM((ncn, 256, nc), BF16),
-            pltpu.VMEM((ncn, 128, nc), BF16),
-            pltpu.VMEM((ncn, 128, nc), F32),
+            pltpu.VMEM((2, 2, 2, 4, 2, 64, HEAD), BF16),
+            pltpu.VMEM((2, 2, 2, 4, 2, 64, HEAD), BF16),
+            pltpu.VMEM((2, QT, 1024), BF16),
+            pltpu.VMEM((2, ncn, 128, nc), BF16),
+            pltpu.VMEM((2, ncn, 128, nc), BF16),
+            pltpu.VMEM((2, ncn, 64, nc), BF16),
+            pltpu.VMEM((ncn, 64, nc), F32),
             dma((kcn,)), dma((2, kcn)), dma((2, kcn)), dma((kcn,)), dma((8,)),
-            dma((2, 2, 2)), dma((2, 2, 2)), dma((2, 2, 2)), dma((2, 2, 2)),
-            dma((ncn,)), dma((ncn,)), dma((ncn,)), dma((ncn,)),
+            dma((2, 2, 2, 2)), dma((2, 2, 2, 2)), dma((2, 2, 2, 2)), dma((2, 2, 2, 2)),
+            dma((2, ncn)), dma((2, ncn)), dma((2, ncn)), dma((2, ncn)),
         ],
         compiler_params=pltpu.CompilerParams(
             collective_id=0, has_side_effects=True, vmem_limit_bytes=60 * 1024 * 1024

time: 82 us -> 80.4 us (0.980)
  Pallas kernels: 80.1 us -> 78.5 us
    pallas_call x1, Pallas kernels: 80.1 us -> 78.5 us  [shards(): pl.pallas_call(functools.partial(kernel, n_ctx, kcn, kc, ncn, nc), out_sh...]
where the time goes in v5:
time: 80.4 us; the launch traced here: 80.3 us
  Pallas kernels  78.5 us (98%)
  other arithmetic  1.76 us (2%)
    pallas_call x1, Pallas kernels, shards(): pl.pallas_call(functools.partial(kernel, n_ctx, kcn, kc, ncn, nc), out_sh...  78.5 us
    add x1, other arithmetic, shards(): return own + across.astype(F32)  1.76 us

profile of v5, /device:TPU:95, one launch (start us, length us, event | category | flops | bytes accessed | tf_op | source)
XLA Modules:
  0.0 80.3 jit_solution(8651087988974680981)
XLA Ops:
  0.0 78.5 %shard_map.64 = (f32[128,5376]{1,0:T(8,128)S(1)}, bf16[128,5376]{1,0:T(8,128)(2,1)S(1)}) custom-call(bf16[512,5376]{1,0:T(8,128)(2,1)} %hid.1, bf16[5376,512]{1,0:T(8,128)(2,1)} %wq.1, bf16[5376,256]{1,0:T(8,128)(2,1)} %wk.1, bf16[5376,256]{1,0:T(8,128)(2,1)} %wv.1, bf16[512,512]{1,0:T(8,128)(2,1)} %dog.1, s32[512]{0:T(512)} %doc.1), custom_call_target="tpu_custom_call" | custom-call | tf_op jit(solution)/shard_map/pallas_call | solution.py:386
  78.5 1.8 %convert_add_fusion = f32[128,5376]{1,0:T(8,128)} fusion(f32[128,5376]{1,0:T(8,128)S(1)} %get-tuple-element.7, bf16[128,5376]{1,0:T(8,128)(2,1)S(1)} %get-tuple-element.8), kind=kLoop, calls=%fused_computation | loop fusion | flops 1376256 | bytes 6881280 | tf_op jit(solution)/shard_map/add | solution.py:422

commit v6 on v5

--- a/solution.py
+++ b/solution.py
@@ -20,6 +20,7 @@
 QT = 256
 KEYS = 1280
 CH = 256
+LAG = 3
 NT = (((1,), (1,)), ((), ()))
 TN = (((0,), (0,)), ((), ()))
 
@@ -351,14 +352,15 @@
             rs1_out[half, c] = part[:128].astype(BF16)
             send_r1(half, c).start()
 
-            @pl.when(c > 0)
+            @pl.when(c >= LAG)
             def _():
-                join(half, c - 1)
+                join(half, c - LAG)
 
             other[c] = part[128:192]
             keep[out_rows(half), out_cols(c)] = part[192:]
 
-        join(half, ncn - 1)
+        for c in range(ncn - LAG, ncn):
+            join(half, c)
 
     @pl.loop(0, ncn)
     def _(c):

time: 80.4 us -> 80.6 us (level)
  no operation moved by 1% of the time
where the time goes in v6:
time: 80.6 us; the launch traced here: 80.2 us
  Pallas kernels  78.4 us (97%)
  other arithmetic  1.76 us (2%)
    pallas_call x1, Pallas kernels, shards(): pl.pallas_call(functools.partial(kernel, n_ctx, kcn, kc, ncn, nc), out_sh...  78.4 us
    add x1, other arithmetic, shards(): return own + across.astype(F32)  1.76 us

profile of v6, /device:TPU:95, one launch (start us, length us, event | category | flops | bytes accessed | tf_op | source)
XLA Modules:
  0.0 80.2 jit_solution(4304053805478721081)
XLA Ops:
  0.0 78.4 %shard_map.64 = (f32[128,5376]{1,0:T(8,128)S(1)}, bf16[128,5376]{1,0:T(8,128)(2,1)S(1)}) custom-call(bf16[512,5376]{1,0:T(8,128)(2,1)} %hid.1, bf16[5376,512]{1,0:T(8,128)(2,1)} %wq.1, bf16[5376,256]{1,0:T(8,128)(2,1)} %wk.1, bf16[5376,256]{1,0:T(8,128)(2,1)} %wv.1, bf16[512,512]{1,0:T(8,128)(2,1)} %dog.1, s32[512]{0:T(512)} %doc.1), custom_call_target="tpu_custom_call" | custom-call | tf_op jit(solution)/shard_map/pallas_call | solution.py:388
  78.5 1.8 %convert_add_fusion = f32[128,5376]{1,0:T(8,128)} fusion(f32[128,5376]{1,0:T(8,128)S(1)} %get-tuple-element.7, bf16[128,5376]{1,0:T(8,128)(2,1)S(1)} %get-tuple-element.8), kind=kLoop, calls=%fused_computation | loop fusion | flops 1376256 | bytes 6881280 | tf_op jit(solution)/shard_map/add | solution.py:424

commit v7 on v6

--- a/solution.py
+++ b/solution.py
@@ -20,7 +20,7 @@
 QT = 256
 KEYS = 1280
 CH = 256
-LAG = 3
+LAG = 2
 NT = (((1,), (1,)), ((), ()))
 TN = (((0,), (0,)), ((), ()))
 
@@ -191,84 +191,124 @@
         for j in range(2):
             relay_kv(0, j)
 
+    def wait_far(g, j):
+        @pl.when(odd == 0)
+        def _():
+            for half in range(2):
+                send_kv(g, j, half, 1).wait_recv()
+
+    def wait_near(g, j):
+        for half in range(2):
+            send_kv(g, j, half, 0).wait_recv()
+
+    def chunk(c):
+        return pl.ds(c * CH, CH)
+
+    near_of = ((2, 3), (1, 2))
+    far_of = ((0, 1), (0,))
+    own_of = ((4,), (3, 4))
+
     @pl.loop(0, 2)
     def _(g):
-        @pl.when(odd == 0)
+        local = lax.broadcasted_iota(jnp.int32, (CH, 2 * QT), 0)
+        lane2 = lax.broadcasted_iota(jnp.int32, (1, QT), 1)
+        edge = jnp.concatenate([lane2, lane2], axis=1)
+        top = [None, None]
+        total, dots = [0.0, 0.0], [0.0, 0.0]
+
+        def keys(j, t, c):
+            return kv[g, j, pl.ds((t + c) * CH, CH), :]
+
+        def score(t, c):
+            kept = lax.dot_general(keys(0, t, c), q[g, t], NT, preferred_element_type=F32)
+            allowed = local >= lo[t] - c * CH
+            if c == 4:
+                allowed = allowed & (local <= edge)
+            kept = jnp.where(allowed, kept, -jnp.inf)
+            s[t, chunk(c), :] = kept
+            here = jnp.max(kept, axis=0, keepdims=True)
+            top[t] = here if top[t] is None else jnp.maximum(top[t], here)
+
+        def weigh(t, c):
+            grads = lax.dot_general(keys(1, t, c), do[g, t], NT, preferred_element_type=F32)
+            weight = jnp.exp2((s[t, chunk(c), :] - top[t]) * (SCALE * LOG2E))
+            s[t, chunk(c), :] = weight
+            dp[t, chunk(c), :] = grads
+            total[t] = total[t] + jnp.sum(weight, axis=0, keepdims=True)
+            dots[t] = dots[t] + jnp.sum(weight * grads, axis=0, keepdims=True)
+
+        def back(t, c, inverse, row_dot):
+            prob = s[t, chunk(c), :] * inverse
+            low_prob = prob.astype(BF16)
+            d_score = (prob * (dp[t, chunk(c), :] - row_dot)).astype(BF16)
+            ds[g, t, chunk(c), :] = d_score
+            if t + c >= 4:
+                pw[g, c - 4 if t == 0 else c - 2] = low_prob
+                return
+            rows = pl.ds((t + c) * CH, CH)
+            d_key = jnp.dot(d_score, q[g, t], preferred_element_type=F32)
+            d_val = jnp.dot(low_prob, do[g, t], preferred_element_type=F32)
+            if t == 1:
+                d_key = d_key + dkv[g, 0, rows, :]
+                d_val = d_val + dkv[g, 1, rows, :]
+            if t == 1 or c == 0:
+                blocks = pl.ds(2 * ((t + c) % 2), 2)
+                split = (2, 2, 64, HEAD)
+                dkv_out[g, 0, (t + c) // 2, blocks] = (d_key * SCALE).astype(BF16).reshape(split)
+                dkv_out[g, 1, (t + c) // 2, blocks] = d_val.astype(BF16).reshape(split)
+            else:
+                dkv[g, 0, rows, :] = d_key
+                dkv[g, 1, rows, :] = d_val
+
+        for t in range(2):
+            for c in own_of[t]:
+                score(t, c)
+        wait_far(g, 0)
+        for t in range(2):
+            for c in far_of[t]:
+                score(t, c)
+        wait_near(g, 0)
+        for t in range(2):
+            for c in near_of[t]:
+                score(t, c)
+        wait_far(g, 1)
+        for t in range(2):
+            for c in own_of[t] + far_of[t]:
+                weigh(t, c)
+
+        @pl.when((odd == 1) & (g == 0))
         def _():
-            for j in range(2):
-                for half in range(2):
-                    send_kv(g, j, half, 1).wait_recv()
-
-        for j in range(2):
-            for half in range(2):
-                send_kv(g, j, half, 0).wait_recv()
-        for t in range(2):
-            lowest = lo[t]
-            local = lax.broadcasted_iota(jnp.int32, (CH, 2 * QT), 0)
-
-            def chunk(c):
-                return pl.ds(c * CH, CH)
-
-            def keys(j, c):
-                return kv[g, j, pl.ds((t + c) * CH, CH), :]
-
-            top = None
-            for c in range(5):
-                kept = lax.dot_general(keys(0, c), q[g, t], NT, preferred_element_type=F32)
-                allowed = local >= lowest - c * CH
-                if c == 4:
-                    lane2 = lax.broadcasted_iota(jnp.int32, (1, QT), 1)
-                    allowed = allowed & (local <= jnp.concatenate([lane2, lane2], axis=1))
-                kept = jnp.where(allowed, kept, -jnp.inf)
-                s[chunk(c), :] = kept
-                here = jnp.max(kept, axis=0, keepdims=True)
-                top = here if top is None else jnp.maximum(top, here)
-
-            total, dots = 0.0, 0.0
-            for c in range(5):
-                grads = lax.dot_general(keys(1, c), do[g, t], NT, preferred_element_type=F32)
-                weight = jnp.exp2((s[chunk(c), :] - top) * (SCALE * LOG2E))
-                s[chunk(c), :] = weight
-                dp[chunk(c), :] = grads
-                total = total + jnp.sum(weight, axis=0, keepdims=True)
-                dots = dots + jnp.sum(weight * grads, axis=0, keepdims=True)
-            inverse = 1.0 / total
-            row_dot = dots * inverse
-
-            for c in range(5):
-                prob = s[chunk(c), :] * inverse
-                low_prob = prob.astype(BF16)
-                d_score = (prob * (dp[chunk(c), :] - row_dot)).astype(BF16)
-                ds[g, t, chunk(c), :] = d_score
-                if t + c < 4:
-                    rows = pl.ds((t + c) * CH, CH)
-                    d_key = jnp.dot(d_score, q[g, t], preferred_element_type=F32)
-                    d_val = jnp.dot(low_prob, do[g, t], preferred_element_type=F32)
-                    if t == 1:
-                        d_key = d_key + dkv[g, 0, rows, :]
-                        d_val = d_val + dkv[g, 1, rows, :]
-                    if t == 1 or c == 0:
-                        blocks = pl.ds(2 * ((t + c) % 2), 2)
-                        split = (2, 2, 64, HEAD)
-                        dkv_out[g, 0, (t + c) // 2, blocks] = (d_key * SCALE).astype(BF16).reshape(split)
-                        dkv_out[g, 1, (t + c) // 2, blocks] = d_val.astype(BF16).reshape(split)
-                    else:
-                        dkv[g, 0, rows, :] = d_key
-                        dkv[g, 1, rows, :] = d_val
-                else:
-                    pw[g, c - 4 if t == 0 else c - 2] = low_prob
-
-            @pl.when((odd == 1) & (g == 0))
-            def _():
-                relay_kv(1, t)
-
+            relay_kv(1, 0)
+
+        wait_near(g, 1)
+        for t in range(2):
+            for c in near_of[t]:
+                weigh(t, c)
+        inverse = [1.0 / total[t] for t in range(2)]
+        row_dot = [dots[t] * inverse[t] for t in range(2)]
+        for t in range(2):
+            for c in near_of[t]:
+                back(t, c, inverse[t], row_dot[t])
+        back(0, 1, inverse[0], row_dot[0])
         for half in range(2):
             for j in range(2):
                 send_dkv(g, j, half, 0).start()
-
-                @pl.when(odd == 0)
-                def _():
+        back(0, 0, inverse[0], row_dot[0])
+        back(1, 0, inverse[1], row_dot[1])
+
+        @pl.when(odd == 0)
+        def _():
+            for half in range(2):
+                for j in range(2):
                     send_dkv(g, j, half, 1).start()
+
+        @pl.when((odd == 1) & (g == 0))
+        def _():
+            relay_kv(1, 1)
+
+        for t in range(2):
+            for c in own_of[t]:
+                back(t, c, inverse[t], row_dot[t])
 
     @pl.loop(0, 2)
     def _(g):
@@ -401,8 +441,8 @@
             pltpu.VMEM((2, 2, 2 * QT, HEAD), BF16),
             pltpu.VMEM((2, 2, 2 * QT, HEAD), BF16),
             pltpu.VMEM((2, 1, 2 * QT), jnp.int32),
-            pltpu.VMEM((KEYS, 2 * QT), F32),
-            pltpu.VMEM((KEYS, 2 * QT), F32),
+            pltpu.VMEM((2, KEYS, 2 * QT), F32),
+            pltpu.VMEM((2, KEYS, 2 * QT), F32),
             pltpu.VMEM((2, 3, CH, 2 * QT), BF16),
             pltpu.VMEM((2, 2, KEYS, 2 * QT), BF16),
             pltpu.VMEM((2, 2, 3 * TOK, HEAD), F32),

time: 80.6 us -> 82.7 us (1.026)
  Pallas kernels: 78.4 us -> 80.6 us
    pallas_call x1, Pallas kernels: 78.4 us -> 80.6 us  [shards(): pl.pallas_call(functools.partial(kernel, n_ctx, kcn, kc, ncn, nc), out_sh...]
where the time goes in v7:
time: 82.7 us; the launch traced here: 82.4 us
  Pallas kernels  80.6 us (97%)
  other arithmetic  1.76 us (2%)
    pallas_call x1, Pallas kernels, shards(): pl.pallas_call(functools.partial(kernel, n_ctx, kcn, kc, ncn, nc), out_sh...  80.6 us
    add x1, other arithmetic, shards(): return own + across.astype(F32)  1.76 us

profile of v7, /device:TPU:95, one launch (start us, length us, event | category | flops | bytes accessed | tf_op | source)
XLA Modules:
  0.0 82.4 jit_solution(12655025761868413706)
XLA Ops:
  0.0 80.6 %shard_map.64 = (f32[128,5376]{1,0:T(8,128)S(1)}, bf16[128,5376]{1,0:T(8,128)(2,1)S(1)}) custom-call(bf16[512,5376]{1,0:T(8,128)(2,1)} %hid.1, bf16[5376,512]{1,0:T(8,128)(2,1)} %wq.1, bf16[5376,256]{1,0:T(8,128)(2,1)} %wk.1, bf16[5376,256]{1,0:T(8,128)(2,1)} %wv.1, bf16[512,512]{1,0:T(8,128)(2,1)} %dog.1, s32[512]{0:T(512)} %doc.1), custom_call_target="tpu_custom_call" | custom-call | tf_op jit(solution)/shard_map/pallas_call | solution.py:428
  80.6 1.8 %convert_add_fusion = f32[128,5376]{1,0:T(8,128)} fusion(f32[128,5376]{1,0:T(8,128)S(1)} %get-tuple-element.7, bf16[128,5376]{1,0:T(8,128)(2,1)S(1)} %get-tuple-element.8), kind=kLoop, calls=%fused_computation | loop fusion | flops 1376256 | bytes 6881280 | tf_op jit(solution)/shard_map/add | solution.py:464

commit v8 on v7

--- a/solution.py
+++ b/solution.py
@@ -290,16 +290,14 @@
             for c in near_of[t]:
                 back(t, c, inverse[t], row_dot[t])
         back(0, 1, inverse[0], row_dot[0])
+        back(0, 0, inverse[0], row_dot[0])
+        back(1, 0, inverse[1], row_dot[1])
         for half in range(2):
             for j in range(2):
                 send_dkv(g, j, half, 0).start()
-        back(0, 0, inverse[0], row_dot[0])
-        back(1, 0, inverse[1], row_dot[1])
-
-        @pl.when(odd == 0)
-        def _():
-            for half in range(2):
-                for j in range(2):
+
+                @pl.when(odd == 0)
+                def _():
                     send_dkv(g, j, half, 1).start()
 
         @pl.when((odd == 1) & (g == 0))

time: 82.7 us -> 83 us (level)
  no operation moved by 1% of the time
where the time goes in v8:
time: 83 us; the launch traced here: 82.5 us
  Pallas kernels  80.8 us (97%)
  other arithmetic  1.76 us (2%)
    pallas_call x1, Pallas kernels, shards(): pl.pallas_call(functools.partial(kernel, n_ctx, kcn, kc, ncn, nc), out_sh...  80.8 us
    add x1, other arithmetic, shards(): return own + across.astype(F32)  1.76 us

profile of v8, /device:TPU:95, one launch (start us, length us, event | category | flops | bytes accessed | tf_op | source)
XLA Modules:
  0.0 82.5 jit_solution(13517165173335720764)
XLA Ops:
  0.0 80.8 %shard_map.64 = (f32[128,5376]{1,0:T(8,128)S(1)}, bf16[128,5376]{1,0:T(8,128)(2,1)S(1)}) custom-call(bf16[512,5376]{1,0:T(8,128)(2,1)} %hid.1, bf16[5376,512]{1,0:T(8,128)(2,1)} %wq.1, bf16[5376,256]{1,0:T(8,128)(2,1)} %wk.1, bf16[5376,256]{1,0:T(8,128)(2,1)} %wv.1, bf16[512,512]{1,0:T(8,128)(2,1)} %dog.1, s32[512]{0:T(512)} %doc.1), custom_call_target="tpu_custom_call" | custom-call | tf_op jit(solution)/shard_map/pallas_call | solution.py:426
  80.8 1.8 %convert_add_fusion = f32[128,5376]{1,0:T(8,128)} fusion(f32[128,5376]{1,0:T(8,128)S(1)} %get-tuple-element.7, bf16[128,5376]{1,0:T(8,128)(2,1)S(1)} %get-tuple-element.8), kind=kLoop, calls=%fused_computation | loop fusion | flops 1376256 | bytes 6881280 | tf_op jit(solution)/shard_map/add | solution.py:462

commit v9 on v5

--- a/solution.py
+++ b/solution.py
@@ -108,8 +108,8 @@
         else:
             source, rows, device = pl.multiple_of(2 * TOK * (1 - odd), TOK), TOK, pair
         return pltpu.make_async_remote_copy(
-            src_ref=kv.at[g, j, pl.ds(source + half * QT, QT), :],
-            dst_ref=kv.at[g, j, pl.ds(rows + half * QT, QT), :],
+            src_ref=kv.at[g, j, pl.ds(source, TOK), :],
+            dst_ref=kv.at[g, j, pl.ds(rows, TOK), :],
             send_sem=kv_ss.at[g, j, half, far],
             recv_sem=kv_rs.at[g, j, half, far],
             device_id=device,
@@ -117,7 +117,7 @@
         )
 
     def relay_kv(g, j):
-        for half in range(2):
+        for half in range(1):
             send_kv(g, j, half, 1).wait_recv()
             send_kv(g, j, half, 0).start()
 
@@ -139,7 +139,7 @@
         if g == 0:
             pl.semaphore_wait(barrier, 5)
         for j in range(2):
-            for half in range(2):
+            for half in range(1):
                 send_kv(g, j, half, 1).start()
 
                 @pl.when(odd == 0)
@@ -195,11 +195,11 @@
         @pl.when(odd == 0)
         def _():
             for j in range(2):
-                for half in range(2):
+                for half in range(1):
                     send_kv(g, j, half, 1).wait_recv()
 
         for j in range(2):
-            for half in range(2):
+            for half in range(1):
                 send_kv(g, j, half, 0).wait_recv()
         for t in range(2):
             lowest = lo[t]
@@ -360,19 +360,20 @@
 
         join(half, ncn - 1)
 
+    for g in range(2):
+        for j in range(2):
+            for half in range(2):
+                for far in range(2):
+                    if half == 0:
+                        send_kv(g, j, half, far).wait_send()
+                    send_dkv(g, j, half, far).wait_send()
+
     @pl.loop(0, ncn)
     def _(c):
         for half in range(2):
             send_r1(half, c).wait_send()
             send_r2(half, c).wait_send()
             send_r2(half, c).wait_recv()
-
-    for g in range(2):
-        for j in range(2):
-            for half in range(2):
-                for far in range(2):
-                    send_kv(g, j, half, far).wait_send()
-                    send_dkv(g, j, half, far).wait_send()
 
 
 def shards(hidden, w_query, key_weight, value_weight, out_gradient, doc_start, *, n_ctx):

time: 80.4 us -> 80.6 us (level)
  no operation moved by 1% of the time
where the time goes in v9:
time: 80.6 us; the launch traced here: 80.4 us
  Pallas kernels  78.7 us (98%)
  other arithmetic  1.76 us (2%)
    pallas_call x1, Pallas kernels, shards(): pl.pallas_call(functools.partial(kernel, n_ctx, kcn, kc, ncn, nc), out_sh...  78.7 us
    add x1, other arithmetic, shards(): return own + across.astype(F32)  1.76 us

profile of v9, /device:TPU:95, one launch (start us, length us, event | category | flops | bytes accessed | tf_op | source)
XLA Modules:
  0.0 80.4 jit_solution(14509410747210278497)
XLA Ops:
  0.0 78.7 %shard_map.64 = (f32[128,5376]{1,0:T(8,128)S(1)}, bf16[128,5376]{1,0:T(8,128)(2,1)S(1)}) custom-call(bf16[512,5376]{1,0:T(8,128)(2,1)} %hid.1, bf16[5376,512]{1,0:T(8,128)(2,1)} %wq.1, bf16[5376,256]{1,0:T(8,128)(2,1)} %wk.1, bf16[5376,256]{1,0:T(8,128)(2,1)} %wv.1, bf16[512,512]{1,0:T(8,128)(2,1)} %dog.1, s32[512]{0:T(512)} %doc.1), custom_call_target="tpu_custom_call" | custom-call | tf_op jit(solution)/shard_map/pallas_call | solution.py:387
  78.7 1.8 %convert_add_fusion = f32[128,5376]{1,0:T(8,128)} fusion(f32[128,5376]{1,0:T(8,128)S(1)} %get-tuple-element.7, bf16[128,5376]{1,0:T(8,128)(2,1)S(1)} %get-tuple-element.8), kind=kLoop, calls=%fused_computation | loop fusion | flops 1376256 | bytes 6881280 | tf_op jit(solution)/shard_map/add | solution.py:423
